TPU v7x, 512 devices: a whole 4x8x8 slice. The times are simulated.
512 devices in a mesh: depth: 16 (over x_hi, z), height: 32 (over x_lo, y, core).
Axes of the slice: x: 4 (x_hi: 2, x_lo: 2; x = x_hi * 2 + x_lo), y: 8, z: 8, core: 2. Of those that a mesh axis runs over, the one named last changes fastest.
Arguments:
- grad_out: bfloat16 [16, 64, 64, 1024], P('depth', 'height'), may hold values from -6 to 6
- pre_act: bfloat16 [16, 64, 64, 1024], P('depth', None, None, 'height'), may hold values from -6 to 6
- w_in: bfloat16 [1024, 1024], P('depth'), may hold values from -0.1875 to 0.1875
- w_out: bfloat16 [1024, 1024], P('depth'), may hold values from -0.1875 to 0.1875
- kernel: bfloat16 [27, 32, 1024], P(None, None, 'height'), may hold values from -0.21875 to 0.21875
Outputs:
- grad_in: bfloat16 [16, 64, 64, 1024], P('depth', 'height')
- kernel_grad: float32 [27, 32, 1024], P(None, None, 'height')
All inputs are finite; a program needn't handle non-finite values.
Results may differ from a plain program's by a relative error of at most 0.014.
Values may be sent and summed in bfloat16 or wider, within the bound.
A program may use at most 64 MiB of HBM per device.

v0:
```python
import jax
import jax.numpy as jnp
from jax import lax
from jax.sharding import PartitionSpec as P


def with_halo(cells, sides, width):
    for axis, dim in sides:
        count = lax.axis_size(axis)
        ends = count - 1
        head = lax.slice_in_dim(cells, 0, width, axis=dim)
        tail = lax.slice_in_dim(cells, cells.shape[dim] - width, cells.shape[dim], axis=dim)
        cells = jnp.concatenate(
            [
                lax.ppermute(tail, axis, [(i, (i + 1) % count) for i in range(ends)]),
                cells,
                lax.ppermute(head, axis, [((i + 1) % count, i) for i in range(ends)]),
            ],
            axis=dim,
        )
    return cells


def shards(grad_out, pre_act, w_in, w_out, kernel):
    product = lax.dot_general(
        grad_out,
        lax.all_gather(w_out, "depth", axis=0, tiled=True),
        (((3,), (1,)), ((), ())),
        preferred_element_type=jnp.float32,
    )
    grad_mid = product.astype(jnp.bfloat16)
    grouped = lax.all_to_all(grad_mid, "height", split_axis=3, concat_axis=1, tiled=True)
    padded = with_halo(grouped, (("depth", 0),), 1)
    padded = jnp.pad(padded, ((0, 0), (1, 1), (1, 1), (0, 0)))
    depth_len, height_len, width_len, chans = pre_act.shape
    group_width = kernel.shape[1]
    groups_here = chans // group_width
    hidden = jnp.maximum(pre_act, jnp.zeros_like(pre_act)).reshape(
        depth_len, height_len, width_len, groups_here, group_width
    )
    kern = kernel.reshape(27, group_width, groups_here, group_width)
    back = jnp.zeros((groups_here, group_width, depth_len, height_len, width_len), jnp.float32)
    grads = []
    for step_d in (-1, 0, 1):
        windows = []
        for step_h in (-1, 0, 1):
            for step_w in (-1, 0, 1):
                windows.append(
                    padded[
                        1 - step_d : 1 - step_d + depth_len,
                        1 - step_h : 1 - step_h + height_len,
                        1 - step_w : 1 - step_w + width_len,
                        :,
                    ]
                )
        stacked = jnp.concatenate(windows, axis=3)
        stacked = stacked.reshape(depth_len, height_len, width_len, 9, groups_here, group_width)
        first = 9 * (step_d + 1)
        kern_plane = kern[first : first + 9]
        back = back + jnp.einsum(
            "dhwkgj,kigj->gidhw", stacked, kern_plane, preferred_element_type=jnp.float32
        )
        grads.append(
            jnp.einsum("dhwkgj,dhwgi->kigj", stacked, hidden, preferred_element_type=jnp.float32)
        )
    back = jnp.transpose(back, (2, 3, 4, 0, 1)).reshape(depth_len, height_len, width_len, chans)
    grad_pre = jnp.where(pre_act > 0, back, jnp.zeros_like(back)).astype(jnp.bfloat16)
    partial_grad = jnp.concatenate(grads, axis=0).reshape(27, group_width, chans)
    total_cells = depth_len * lax.axis_size("depth") * height_len * width_len
    scale = jnp.float32(total_cells) ** (-0.5)
    kernel_grad = lax.psum(partial_grad.astype(jnp.bfloat16), "depth").astype(jnp.float32) * scale
    by_height = lax.all_to_all(grad_pre, "height", split_axis=1, concat_axis=3, tiled=True)
    branch = lax.dot_general(
        by_height,
        lax.all_gather(w_in, "depth", axis=0, tiled=True),
        (((3,), (1,)), ((), ())),
        preferred_element_type=jnp.float32,
    )
    grad_in = (grad_out.astype(jnp.float32) + branch).astype(jnp.bfloat16)
    return (grad_in, kernel_grad)


def solution(mesh):
    in_specs = (
        P("depth", "height", None, None),
        P("depth", None, None, "height"),
        P("depth", None),
        P("depth", None),
        P(None, None, "height"),
    )
    out_specs = (P("depth", "height", None, None), P(None, None, "height"))
    return jax.shard_map(shards, mesh=mesh, in_specs=in_specs, out_specs=out_specs, check_vma=False)
```

profile of v0, /device:TPU:6, one launch (start us, length us, event | category | flops | bytes accessed | tf_op | source)
XLA Modules:
  0.0 285.2 jit_solution(9083214202270990740)
XLA Ops:
  7.2 0.0 all-gather.3.cloned.1.call-start
  7.2 0.7 all-gather.3.cloned.1.call-update
  7.9 0.0 all-gather.5.cloned.1.call-start
  7.9 97.8 %all-gather.3.cloned.1.call-done = bf16[1024,1024]{1,0:T(8,128)(2,1)} async-done(((bf16[64,1024]{1,0:T(8,128)(2,1)}), bf16[1024,1024]{1,0:T(8,128)(2,1)}) %all-gather.3.cloned.1.call-update) | async-done | bytes 2097168 | tf_op jit(solution)/shard_map/all_gather | solution.py:27
  105.7 2.5 fusion.28
  108.2 0.4 copy.18
  108.6 0.4 reshape.89
  109.0 20.0 %all_to_all.33 = bf16[32,2,2048]{2,1,0:T(2,128)(2,1)S(1)} all-to-all(bf16[32,2,2048]{2,1,0:T(2,128)(2,1)S(1)} %reshape.89), channel_id=1, replica_groups=mesh['depth'=16,'height'=32] {'height'}, dimensions={0} | all-to-all | bytes 524288 | tf_op jit(solution)/shard_map/all_to_all | solution.py:32
  129.0 0.4 reshape.90
  129.3 0.1 copy.19
  129.4 0.1 copy.20
  129.5 2.8 collective-permute-start
  132.3 6.6 %collective-permute-start.1 = (bf16[1,64,64,32]{2,3,1,0:T(8,128)(2,1)S(1)}, bf16[1,64,64,32]{2,3,1,0:T(8,128)(2,1)S(1)}, u32[]{:S(2)}, u32[]{:S(2)}) collective-permute-start(bf16[1,64,64,32]{2,3,1,0:T(8,128)(2,1)S(1)} %bitcast.164), channel_id=1, source_target_pairs={{32,0},{64,32},{96,64},{128,96},{160,128},{192,160},{224,192},{256... | collective-permute-start | bytes 786440 | tf_op jit(solution)/shard_map/ppermute | solution.py:17
  139.0 0.0 all-gather.5.cloned.1.call-update
  139.0 8.8 %collective-permute-done = bf16[1,64,64,32]{2,3,1,0:T(8,128)(2,1)S(1)} collective-permute-done((bf16[1,64,64,32]{2,3,1,0:T(8,128)(2,1)S(1)}, bf16[1,64,64,32]{2,3,1,0:T(8,128)(2,1)S(1)}, u32[]{:S(2)}, u32[]{:S(2)}) %collective-permute-start) | collective-permute-done | bytes 262176 | tf_op jit(solution)/shard_map/ppermute | solution.py:15
  147.8 1.9 collective-permute-done.1
  149.7 1.3 select_maximum_fusion
  150.9 1.2 slice_dynamic-update-slice_fusion.23
  152.1 1.5 slice_dynamic-update-slice_fusion.22
  153.6 1.3 slice_dynamic-update-slice_fusion.21
  154.9 1.4 slice_dynamic-update-slice_fusion.20
  156.4 1.1 constant_dynamic-update-slice_fusion
  157.5 1.4 slice_dynamic-update-slice_fusion.19
  158.9 0.1 constant_dynamic-update-slice_fusion.2
  158.9 0.0 copy-start.4
  158.9 1.4 slice_dynamic-update-slice_fusion.18
  160.3 1.5 slice_dynamic-update-slice_fusion.17
  161.9 1.3 slice_dynamic-update-slice_fusion.16
  163.2 0.1 slice_dynamic-update-slice_fusion
  163.3 0.0 copy-start.2
  163.3 1.2 convolution_bitcast_fusion
  164.5 5.6 %convolution_bitcast_fusion.1 = f32[64,64,32]{1,2,0:T(8,128)S(1)} fusion(bf16[64,64,9,32]{1,3,2,0:T(8,128)(2,1)} %bitcast.10, bf16[27,32,32]{2,1,0:T(8,128)(2,1)S(1)} %copy-done.4), kind=kOutput, calls=%fused_computation.17 | convolution fusion | flops 75497472 | bytes 2957312 | tf_op jit(solution)/shard_map/dhwkgj,kigj->gidhw/dot_general | solution.py:60
  170.1 0.0 copy-done.1
  170.2 0.0 copy-done.2
  170.2 1.2 fusion.56
  171.4 1.1 reshape.91
  172.5 5.1 %all-to-all-start.1 = ((bf16[32,2,2048]{2,1,0:T(2,128)(2,1)}), bf16[32,2,2048]{2,1,0:T(2,128)(2,1)S(1)}, u32[]{:S(2)}, u32[]{:S(2)}) async-start(bf16[32,2,2048]{2,1,0:T(2,128)(2,1)} %reshape.91), calls=%async_computation.1 | async-start | bytes 524288 | tf_op jit(solution)/shard_map/all_to_all | solution.py:72
  177.6 0.0 slice-start.1
  177.6 5.8 %fusion.34 = bf16[9,32,1,32]{3,1,0,2:T(8,128)(2,1)S(1)} fusion(bf16[64,64,9,32]{1,3,2,0:T(8,128)(2,1)} %bitcast.158, bf16[1,64,64,32]{2,3,1,0:T(8,128)(2,1)S(1)} %copy-done.2), kind=kOutput, calls=%fused_computation.36 | convolution fusion | flops 76030976 | bytes 2639872 | tf_op jit(solution)/shard_map/dhwkgj,dhwgi->kigj/dot_general | solution.py:64
  183.4 5.6 %fusion.35 = bf16[9,32,1,32]{3,1,0,2:T(8,128)(2,1)S(1)} fusion(bf16[64,64,9,32]{1,3,2,0:T(8,128)(2,1)} %bitcast.10, bf16[1,64,64,32]{2,3,1,0:T(8,128)(2,1)S(1)} %copy-done.2), kind=kOutput, calls=%fused_computation.37 | convolution fusion | flops 76030976 | bytes 2639872 | tf_op jit(solution)/shard_map/dhwkgj,dhwgi->kigj/dot_general | solution.py:64
  189.1 0.0 copy-start.3
  189.1 3.4 %fusion.36 = bf16[9,32,1,32]{3,1,0,2:T(8,128)(2,1)S(1)} fusion(bf16[64,64,9,32]{1,3,2,0:T(8,128)(2,1)S(1)} %bitcast.162, bf16[1,64,64,32]{2,3,1,0:T(8,128)(2,1)S(1)} %copy-done.2), kind=kOutput, calls=%fused_computation.38 | convolution fusion | flops 76030976 | bytes 2639872 | tf_op jit(solution)/shard_map/dhwkgj,dhwgi->kigj/dot_general | solution.py:64
  192.5 0.1 maximum_bitcast_fusion
  192.5 81.4 %psum.7 = bf16[27,32,32]{2,1,0:T(8,128)(2,1)S(1)} all-reduce(bf16[27,32,32]{2,1,0:T(8,128)(2,1)S(1)} %maximum_bitcast_fusion), channel_id=1, replica_groups=mesh['depth'=16,'height'=32] {'depth'}, use_global_device_ids=true, to_apply=%region_0.1 | all-reduce | flops 27648 | bytes 110592 | tf_op jit(solution)/shard_map/psum | solution.py:71
  273.9 0.8 convert_multiply_fusion
  274.8 0.4 reshape.92
  275.2 0.0 all-gather.5.cloned.1.call-done
  275.2 3.2 %fusion.25 = bf16[1,2,64,1024]{3,2,1,0:T(8,128)(2,1)} fusion(bf16[2,64,1024]{1,2,0:T(8,128)(2,1)S(1)} %bitcast.171, bf16[1024,1024]{1,0:T(8,128)(2,1)} %all-gather.5.cloned.1.call-done, bf16[1,2,64,1024]{3,2,1,0:T(8,128)(2,1)S(1)} %copy-done.3), kind=kOutput, calls=%fused_computation.28 | convolution fusion | flops 268828672 | bytes 2883584 | tf_op jit(solution)/shard_map/dot_general | solution.py:73
  (11 shorter events, 0.1 us)
Async XLA Ops:
  7.2 98.6 %all-gather.3.cloned.1.call-start = ((), (), s32[]{:S(2)}) async-start(), calls=%async_computation.2 | async-start | bytes 2228224 | tf_op jit(solution)/shard_map/all_gather | solution.py:27
  7.9 267.3 %all-gather.5.cloned.1.call-start = ((), (), s32[]{:S(2)}) async-start(), calls=%async_computation.3 | async-start | bytes 2228224 | tf_op jit(solution)/shard_map/all_gather | solution.py:75
  129.5 18.3 %collective-permute-start = (bf16[1,64,64,32]{2,3,1,0:T(8,128)(2,1)S(1)}, bf16[1,64,64,32]{2,3,1,0:T(8,128)(2,1)S(1)}, u32[]{:S(2)}, u32[]{:S(2)}) collective-permute-start(bf16[1,64,64,32]{2,3,1,0:T(8,128)(2,1)S(1)} %bitcast.163), channel_id=1, source_target_pairs={{0,32},{32,64},{64,96},{96,128},{128,160},{160,192},{192,224},{224... | collective-permute-start | bytes 786440 | tf_op jit(solution)/shard_map/ppermute | solution.py:15
  132.3 17.3 %collective-permute-start.1 = (bf16[1,64,64,32]{2,3,1,0:T(8,128)(2,1)S(1)}, bf16[1,64,64,32]{2,3,1,0:T(8,128)(2,1)S(1)}, u32[]{:S(2)}, u32[]{:S(2)}) collective-permute-start(bf16[1,64,64,32]{2,3,1,0:T(8,128)(2,1)S(1)} %bitcast.164), channel_id=1, source_target_pairs={{32,0},{64,32},{96,64},{128,96},{160,128},{192,160},{224,192},{256... | collective-permute-start | bytes 786440 | tf_op jit(solution)/shard_map/ppermute | solution.py:17
  158.9 4.4 %copy-start.4 = (bf16[27,32,32]{2,1,0:T(8,128)(2,1)S(1)}, bf16[27,32,32]{2,1,0:T(8,128)(2,1)}, u32[]{:S(2)}) copy-start(bf16[27,32,32]{2,1,0:T(8,128)(2,1)} %param.9) | copy-start | bytes 165892
  163.2 6.9 %copy-start.1 = (bf16[1,64,64,288]{2,3,1,0:T(8,128)(2,1)}, bf16[1,64,64,288]{2,3,1,0:T(8,128)(2,1)S(1)}, u32[]{:S(2)}) copy-start(bf16[1,64,64,288]{2,3,1,0:T(8,128)(2,1)S(1)} %get-tuple-element.2) | copy-start | bytes 7077892
  163.3 6.8 %copy-start = (bf16[1,64,64,288]{2,3,1,0:T(8,128)(2,1)}, bf16[1,64,64,288]{2,3,1,0:T(8,128)(2,1)S(1)}, u32[]{:S(2)}) copy-start(bf16[1,64,64,288]{2,3,1,0:T(8,128)(2,1)S(1)} %slice_dynamic-update-slice_fusion) | copy-start | bytes 7077892
  163.3 6.8 %copy-start.2 = (bf16[1,64,64,32]{2,3,1,0:T(8,128)(2,1)S(1)}, bf16[1,64,64,32]{2,3,1,0:T(8,128)(2,1)}, u32[]{:S(2)}) copy-start(bf16[1,64,64,32]{2,3,1,0:T(8,128)(2,1)} %param.6) | copy-start | bytes 786436
  172.5 16.5 %slice-start = ((s8[4718592]{0:T(1024)(128)(4,1)}), s8[524288]{0:T(1024)(128)(4,1)S(1)}, s32[]{:S(2)}) async-start(s8[4718592]{0:T(1024)(128)(4,1)} %bitcast.160), calls=%async_computation.4 | async-start | bytes 1048576
  172.5 102.2 %all-to-all-start.1 = ((bf16[32,2,2048]{2,1,0:T(2,128)(2,1)}), bf16[32,2,2048]{2,1,0:T(2,128)(2,1)S(1)}, u32[]{:S(2)}, u32[]{:S(2)}) async-start(bf16[32,2,2048]{2,1,0:T(2,128)(2,1)} %reshape.91), calls=%async_computation.1 | async-start | bytes 524288 | tf_op jit(solution)/shard_map/all_to_all | solution.py:72
  177.6 11.5 %slice-start.1 = ((s8[4718592]{0:T(1024)(128)(4,1)}), s8[4194304]{0:T(1024)(128)(4,1)S(1)}, s32[]{:S(2)}) async-start(s8[4718592]{0:T(1024)(128)(4,1)} %bitcast.160), calls=%async_computation.5 | async-start | bytes 8388608
  189.1 86.1 %copy-start.3 = (bf16[1,2,64,1024]{3,2,1,0:T(8,128)(2,1)S(1)}, bf16[1,2,64,1024]{3,2,1,0:T(8,128)(2,1)}, u32[]{:S(2)}) copy-start(bf16[1,2,64,1024]{3,2,1,0:T(8,128)(2,1)} %param.5) | copy-start | bytes 786436
Sparse Core Ops, SparseCore 0:
  11.1 94.5 all-gather.2
  139.1 84.1 all-gather.4
where the time goes:
time: 286 us; the launch traced here: 285 us
  waiting for transfers between devices  109 us (38%)
  blocking collectives  101 us (35%)
  matrix products  28.5 us (10%)
  local copies, waits for them, and re-layouts  15.2 us (5%)
  starting transfers between devices  14.6 us (5%)
  between operations  14.3 us (5%)
    all_gather x1, waiting for transfers between devices, shards(): lax.all_gather(w_out, 'depth', axis=0, tiled=True)  97.8 us
    psum x1, blocking collectives, shards(): lax.psum(partial_grad.astype(jnp.bfloat16), 'depth').astype(jnp.float32)  81.4 us
    all_to_all x1, blocking collectives, shards(): lax.all_to_all(grad_mid, 'height', split_axis=3, concat_axis=1, tiled=True)  20 us
    dot_general x3, matrix products, shards(): jnp.einsum('dhwkgj,dhwgi->kigj', stacked, hidden, preferred_element_type=...  14.8 us
    unnamed x27, local copies, waits for them, and re-layouts  13.2 us
    ppermute x1, waiting for transfers between devices, with_halo(): lax.ppermute(tail, axis, [(i, (i + 1) % count) for i in range(ends)])  8.79 us
    dot_general x3, matrix products, shards(): jnp.einsum('dhwkgj,kigj->gidhw', stacked, kern_plane, preferred_element_t...  8.03 us
    ppermute x1, starting transfers between devices, with_halo(): lax.ppermute(head, axis, [((i + 1) % count, i) for i in range(ends)])  6.61 us
  transfers between devices with their start and end apart: 5, of which 3 were waited for; matrix products, arithmetic and copies ran while one was open for 14% of the time, Pallas kernels for 0%

commit v1 on v0

v1 whole, which is shorter than its diff:
```python
import functools

import jax
import jax.numpy as jnp
from jax import lax
from jax.experimental import pallas as pl
from jax.experimental.pallas import tpu as pltpu
from jax.sharding import PartitionSpec as P

MESH = pl.DeviceIdType.MESH
BF = jnp.bfloat16
F32 = jnp.float32


def body(
    DN, C,
    go_ref, pre_ref, wi_ref, wo_ref, kern_ref,
    out_ref, kg_ref,
    go_buf, wo_buf, wi_buf, wi_own, mt_buf, m_buf, xa, xb, pre2, kmf, kmat, acc, gp_stage, gpr,
    gbuf, g_stage, g_recv, g_fin, p_send, p_recv,
    go_sem, wo_s, wo_r, wi_s, wi_r, a1_s, a1_r, h_s, h_r, a2_s, a2_r, rs_s, rs_r, ag_s, ag_r, p_s, p_r,
):
    HN = 2 * DN
    Z = DN // 2
    HALF = Z // 2
    NQ = HN // 4
    NCH = h_s.shape[1]
    KPC = DN // NCH
    SPD = g_stage.shape[1]
    NP = p_send.shape[0]
    PW = C // NP

    d = lax.axis_index("depth")
    h = lax.axis_index("height")
    k = h // 2
    c = h % 2
    xh = d // Z
    z = d % Z

    def remote(src, dst, ss, rs, dd, hh):
        return pltpu.make_async_remote_copy(
            src_ref=src, dst_ref=dst, send_sem=ss, recv_sem=rs, device_id=(dd, hh), device_id_type=MESH
        )

    partner = 2 * k + (1 - c)

    barrier = pltpu.get_barrier_semaphore()
    pl.semaphore_signal(barrier, inc=1, device_id=(d, partner), device_id_type=MESH)

    @pl.loop(1, DN)
    def _(j):
        pl.semaphore_signal(barrier, inc=1, device_id=((d + j) % DN, h), device_id_type=MESH)
        pl.semaphore_signal(barrier, inc=1, device_id=(d, 2 * ((k + j) % DN) + c), device_id_type=MESH)

    zero_tile = jnp.zeros((32, 128), BF)
    for s in range(3):
        m_buf[s, 0] = zero_tile
        m_buf[s, HN + 1] = zero_tile

    @pl.when(d == 0)
    def _():
        m_buf[2] = jnp.zeros(m_buf.shape[1:], BF)

    @pl.when(d == DN - 1)
    def _():
        m_buf[0] = jnp.zeros(m_buf.shape[1:], BF)

    go_buf[pl.ds(pl.multiple_of(128 * c, 128), 128), :] = go_ref[...]

    for o in range(27):
        s, m = divmod(o, 9)
        kmf[s, :, 32 * m : 32 * m + 32] = kern_ref[o].astype(F32)
    for s in range(3):
        kmat[s] = kmf[s].astype(BF)

    @pl.loop(0, HN)
    def _(t):
        both = jnp.concatenate([pre_ref[2 * t].astype(F32), pre_ref[2 * t + 1].astype(F32)], axis=1)
        pre2[t] = both.astype(BF)

    col = lax.broadcasted_iota(jnp.int32, (C, C // 2), 1)
    row = lax.broadcasted_iota(jnp.int32, (C, C // 2), 0)
    pick = jnp.where(row == 64 * (col // 32) + 32 * c + col % 32, 1.0, 0.0).astype(BF)
    wi_own[...] = jnp.dot(wi_ref[...], pick, preferred_element_type=F32).astype(BF)

    pl.semaphore_wait(barrier, 1 + 2 * (DN - 1))

    go_copy = remote(
        go_ref, go_buf.at[pl.ds(pl.multiple_of(128 * c, 128), 128), :], go_sem.at[0], go_sem.at[1], d, partner
    )
    go_copy.start()

    class Ring:
        def __init__(self, own, buf, ss, rs):
            self.own, self.buf, self.ss, self.rs = own, buf, ss, rs
            self.sent = []

        def idx(self, far, dz):
            side = 1 - xh if far else xh
            return side * Z + (z + dz + Z) % Z

        def send(self, far, dz, step):
            i = self.idx(far, dz)
            src = self.own if (not far and dz == 0) else self.buf.at[i]
            copy = remote(
                src, self.buf.at[i], self.ss.at[len(self.sent)], self.rs.at[i], xh * Z + (z + step + Z) % Z, h
            )
            copy.start()
            self.sent.append(copy)

        def begin(self):
            if HALF >= 1:
                self.send(False, 0, 1)
            copy = remote(
                self.own, self.buf.at[d], self.ss.at[len(self.sent)], self.rs.at[d], (1 - xh) * Z + z, h
            )
            copy.start()
            self.sent.append(copy)
            if HALF - 1 >= 1:
                self.send(False, 0, -1)

        def take(self, far, dz):
            i = self.idx(far, dz)
            remote(self.buf.at[i], self.buf.at[i], self.ss.at[0], self.rs.at[i], d, partner).wait_recv()
            return i

        def arrivals(self, s):
            if s == 0:
                return [(True, 0, 0)]
            out = []
            if s <= HALF:
                out.append((False, -s, 1))
            if s <= HALF:
                out.append((True, s, -1))
            if s <= HALF - 1:
                out.append((False, s, -1))
                out.append((True, -s, 1))
            return out

        def pump(self, s, work=None):
            for far, dz, step in self.arrivals(s):
                i = self.take(far, dz)
                if s == 0:
                    if HALF >= 1:
                        self.send(True, 0, -1)
                    if HALF - 1 >= 1:
                        self.send(True, 0, 1)
                else:
                    limit = HALF if (far == (step < 0)) else HALF - 1
                    if s + 1 <= limit:
                        self.send(far, dz, step)
                if work is not None:
                    work(i)

        def finish(self):
            for copy in self.sent:
                copy.wait_send()

    own_rows = wo_ref.at[pl.ds(pl.multiple_of(32 * c, 32), 32), :]
    ring_o = Ring(own_rows, wo_buf, wo_s, wo_r)
    ring_i = Ring(wi_own, wi_buf, wi_s, wi_r)
    ring_o.begin()

    def project(block, i):
        mid = lax.dot_general(block, go_buf[...], (((1,), (1,)), ((), ())), preferred_element_type=F32)
        mid = mid.astype(BF)

        @pl.when(i == k)
        def _():
            m_buf[1, 1 + 2 * i] = mid[:, :128]
            m_buf[1, 2 + 2 * i] = mid[:, 128:]

        @pl.when(i != k)
        def _():
            mt_buf[i, 0] = mid[:, :128]
            mt_buf[i, 1] = mid[:, 128:]
            remote(
                mt_buf.at[i], m_buf.at[1, pl.ds(1 + 2 * k, 2)], a1_s.at[i], a1_r.at[k], d, 2 * i + c
            ).start()

    go_copy.wait_recv()
    project(own_rows[...], d)
    for s in range(HALF + 1):
        ring_o.pump(s, lambda i: project(wo_buf[i], i))

    up, down = jnp.minimum(d + 1, DN - 1), jnp.maximum(d - 1, 0)

    def halo(n, side):
        part = pl.ds(1 + 2 * KPC * n, 2 * KPC)
        return remote(
            m_buf.at[1, part],
            m_buf.at[2 if side == 0 else 0, part],
            h_s.at[side, n],
            h_r.at[side, n],
            up if side == 0 else down,
            h,
        )

    for n in range(NCH):
        for j in range(KPC):
            i = KPC * n + j

            @pl.when(i != k)
            def _(i=i):
                part = m_buf.at[1, pl.ds(1 + 2 * i, 2)]
                remote(part, part, a1_s.at[0], a1_r.at[i], d, partner).wait_recv()

        @pl.when(d < DN - 1)
        def _(n=n):
            halo(n, 0).start()

        @pl.when(d > 0)
        def _(n=n):
            halo(n, 1).start()

    ring_i.begin()

    lane = lax.broadcasted_iota(jnp.int32, (4, 32, 128), 2)
    low = lane < 64
    first = lane % 64 == 0
    last = lane % 64 == 63

    def widen(dst, s, at, n, v):
        v0 = v[:n]
        zero = jnp.zeros_like(v0)
        dst[s, pl.ds(at, n), 0:32, :] = jnp.where(last[:n], zero, pltpu.roll(v0, 127, 2)).astype(BF)
        dst[s, pl.ds(at, n), 32:64, :] = v0.astype(BF)
        dst[s, pl.ds(at, n), 64:96, :] = jnp.where(first[:n], zero, pltpu.roll(v0, 1, 2)).astype(BF)

    def spread(s):
        @pl.loop(0, NQ)
        def _(q):
            here = m_buf[s, pl.ds(1 + 4 * q, 4)].astype(F32)
            before = m_buf[s, pl.ds(4 * q, 4)].astype(F32)
            widen(xa, s, 4 * q, 4, here)
            widen(xb, s, 4 * q, 4, jnp.where(low, pltpu.roll(before, 64, 2), pltpu.roll(here, 64, 2)))

        end = m_buf[s, pl.ds(HN, 1)].astype(F32)
        widen(xb, s, HN, 1, jnp.where(low[:1], pltpu.roll(end, 64, 2), jnp.zeros_like(end)))

    def columns(s, q):
        tiles = []
        for j in range(4):
            t = 4 * q + j
            tiles.append(jnp.concatenate([xb[s, t + 1], xa[s, t], xb[s, t]], axis=0))
        return jnp.concatenate(tiles, axis=1)

    def hidden(q):
        tiles = [jnp.maximum(pre2[4 * q + j], jnp.zeros((32, 128), BF)) for j in range(4)]
        return jnp.concatenate(tiles, axis=1)

    def outer(x, q):
        return lax.dot_general(hidden(q), x, (((1,), (1,)), ((), ())), preferred_element_type=F32)

    gbuf[...] = jnp.zeros_like(gbuf)

    spread(1)

    @pl.loop(0, NQ)
    def _(q):
        x = columns(1, q)
        acc[q] = jnp.dot(kmat[1], x, preferred_element_type=F32)
        gbuf[1, :, 0:288] += outer(x, q)

    ring_i.pump(0)
    ring_i.pump(1)

    for n in range(NCH):
        @pl.when(d < DN - 1)
        def _(n=n):
            halo(n, 1).wait_recv()

        @pl.when(d > 0)
        def _(n=n):
            halo(n, 0).wait_recv()

    spread(0)
    spread(2)
    if HALF >= 2:
        ring_i.pump(2)

    @pl.loop(0, NQ)
    def _(p):
        q = (p + k // 2) % NQ
        back = acc[q] + jnp.dot(kmat[0], columns(0, q), preferred_element_type=F32)
        back = back + jnp.dot(kmat[2], columns(2, q), preferred_element_type=F32)
        for j in range(4):
            gate = pre2[4 * q + j].astype(F32) > 0
            tile = jnp.where(gate, back[:, 128 * j : 128 * j + 128], jnp.zeros((32, 128), F32))
            gp_stage[4 * q + j] = tile.astype(BF)
        for j in range(2):
            i = 2 * q + j

            @pl.when(i == k)
            def _(i=i):
                for t in range(2):
                    gpr[t, pl.ds(pl.multiple_of(32 * k, 32), 32), :] = gp_stage[2 * i + t]

            @pl.when(i != k)
            def _(i=i):
                remote(
                    gp_stage.at[pl.ds(2 * i, 2)],
                    gpr.at[:, pl.ds(pl.multiple_of(32 * k, 32), 32), :],
                    a2_s.at[i],
                    a2_r.at[k],
                    d,
                    2 * i + c,
                ).start()

    if HALF >= 3:
        ring_i.pump(3)

    @pl.loop(0, NQ)
    def _(q):
        gbuf[0, :, 0:288] += outer(columns(0, q), q)
        gbuf[2, :, 0:288] += outer(columns(2, q), q)

    def slot(f):
        return f // SPD, f % SPD

    def cut(f):
        s, rest = divmod(f, 12)
        rb, lt = divmod(rest, 3)
        return s, slice(8 * rb, 8 * rb + 8), slice(128 * lt, 128 * lt + 128)

    for f in range(SPD * DN):
        a, b = slot(f)
        g_stage[a, b] = gbuf[cut(f)].astype(BF) if f < 36 else jnp.zeros((8, 128), BF)

    @pl.loop(1, DN)
    def _(j):
        r = (d + j) % DN
        remote(g_stage.at[r], g_recv.at[d], rs_s.at[r], rs_r.at[d], r, h).start()

    for s in range(4, HALF + 1):
        ring_i.pump(s)
    wi_buf[d] = wi_own[...]

    @pl.loop(1, DN)
    def _(j):
        i = (k + j) % DN
        part = gpr.at[:, pl.ds(pl.multiple_of(32 * i, 32), 32), :]
        remote(part, part, a2_s.at[0], a2_r.at[i], d, partner).wait_recv()

    rows_p = wi_buf.shape[0] // NP

    def half(cells, n):
        w = wi_buf[rows_p * n : rows_p * (n + 1)].reshape(PW, C // 2)
        return lax.dot_general(cells, w, (((1,), (1,)), ((), ())), preferred_element_type=F32)

    theirs = gpr[1 - c].T
    exchange = []
    for n in range(NP):
        p_send[n] = half(theirs, n)
        copy = remote(p_send.at[n], p_recv.at[n], p_s.at[n], p_r.at[n], d, partner)
        copy.start()
        exchange.append(copy)

    total = g_stage[d].astype(F32)
    for j in range(1, DN):
        r = (d + j) % DN
        remote(g_recv.at[r], g_recv.at[r], rs_s.at[0], rs_r.at[r], d, partner).wait_recv()
        total = total + g_recv[r].astype(F32)
    g_fin[d] = total.astype(BF)

    @pl.loop(1, DN)
    def _(j):
        r = (d + j) % DN
        remote(g_fin.at[d], g_fin.at[d], ag_s.at[r], ag_r.at[d], r, h).start()

    mine = gpr[c].T
    for n in range(NP):
        part = half(mine, n)
        exchange[n].wait_recv()
        cols = slice(PW * n, PW * (n + 1))
        out_ref[:, cols] = (go_ref[:, cols].astype(F32) + (part + p_recv[n])).astype(BF)

    @pl.loop(1, DN)
    def _(j):
        r = (d + j) % DN
        remote(g_fin.at[r], g_fin.at[r], ag_s.at[0], ag_r.at[r], d, partner).wait_recv()

    scale = float(DN * 2 * HN * 64) ** -0.5
    for f in range(36):
        gbuf[cut(f)] = g_fin[slot(f)].astype(F32) * scale
    for o in range(27):
        s, m = divmod(o, 9)
        kg_ref[o] = gbuf[s, :, 32 * m : 32 * m + 32]

    go_copy.wait_send()
    ring_o.finish()
    ring_i.finish()
    for copy in exchange:
        copy.wait_send()
    for n in range(NCH):
        @pl.when(d < DN - 1)
        def _(n=n):
            halo(n, 0).wait_send()

        @pl.when(d > 0)
        def _(n=n):
            halo(n, 1).wait_send()

    @pl.loop(1, DN)
    def _(j):
        i = (k + j) % DN
        r = (d + j) % DN
        remote(mt_buf.at[i], mt_buf.at[i], a1_s.at[i], a1_r.at[i], d, partner).wait_send()
        part = gp_stage.at[pl.ds(2 * i, 2)]
        remote(part, part, a2_s.at[i], a2_r.at[i], d, partner).wait_send()
        remote(g_stage.at[r], g_recv.at[r], rs_s.at[r], rs_r.at[r], d, partner).wait_send()
        remote(g_fin.at[d], g_fin.at[d], ag_s.at[r], ag_r.at[r], d, partner).wait_send()


def shards(DN, grad_out, pre_act, w_in, w_out, kernel):
    C = grad_out.shape[-1]
    HN = 2 * DN
    rows = grad_out.reshape(128, C)
    turned = jnp.transpose(pre_act, (0, 1, 3, 2)).reshape(2 * HN, 32, 64)
    nch = max(1, DN // 4)
    spd = -(-36 // DN)
    np_ = max(1, C // 256)
    sends = DN
    dma = pltpu.SemaphoreType.DMA
    vmem = pl.BlockSpec(memory_space=pltpu.VMEM)
    grad_in, kernel_grad = pl.pallas_call(
        functools.partial(body, DN, C),
        out_shape=(
            jax.ShapeDtypeStruct((128, C), BF),
            jax.ShapeDtypeStruct((27, 32, 32), F32),
        ),
        in_specs=[vmem] * 5,
        out_specs=(vmem, vmem),
        scratch_shapes=[
            pltpu.VMEM((256, C), BF),
            pltpu.VMEM((DN, 32, C), BF),
            pltpu.VMEM((DN, 64, C // 2), BF),
            pltpu.VMEM((64, C // 2), BF),
            pltpu.VMEM((DN, 2, 32, 128), BF),
            pltpu.VMEM((3, HN + 2, 32, 128), BF),
            pltpu.VMEM((3, HN, 96, 128), BF),
            pltpu.VMEM((3, HN + 1, 96, 128), BF),
            pltpu.VMEM((HN, 32, 128), BF),
            pltpu.VMEM((3, 32, 288), F32),
            pltpu.VMEM((3, 32, 288), BF),
            pltpu.VMEM((HN // 4, 32, 512), F32),
            pltpu.VMEM((HN, 32, 128), BF),
            pltpu.VMEM((2, C // 2, 128), BF),
            pltpu.VMEM((3, 32, 384), F32),
            pltpu.VMEM((DN, spd, 8, 128), BF),
            pltpu.VMEM((DN, spd, 8, 128), BF),
            pltpu.VMEM((DN, spd, 8, 128), BF),
            pltpu.VMEM((np_, 128, C // np_), F32),
            pltpu.VMEM((np_, 128, C // np_), F32),
            dma((2,)),
            dma((sends,)),
            dma((DN,)),
            dma((sends,)),
            dma((DN,)),
            dma((DN,)),
            dma((DN,)),
            dma((2, nch)),
            dma((2, nch)),
            dma((DN,)),
            dma((DN,)),
            dma((DN,)),
            dma((DN,)),
            dma((DN,)),
            dma((DN,)),
            dma((np_,)),
            dma((np_,)),
        ],
        compiler_params=pltpu.CompilerParams(
            collective_id=0, has_side_effects=True, vmem_limit_bytes=48 << 20
        ),
    )(rows, turned, w_in, w_out, kernel)
    return grad_in.reshape(grad_out.shape), kernel_grad


def solution(mesh):
    in_specs = (
        P("depth", "height", None, None),
        P("depth", None, None, "height"),
        P("depth", None),
        P("depth", None),
        P(None, None, "height"),
    )
    out_specs = (P("depth", "height", None, None), P(None, None, "height"))
    step = functools.partial(shards, mesh.shape["depth"])
    return jax.shard_map(step, mesh=mesh, in_specs=in_specs, out_specs=out_specs, check_vma=False)
```

time: 286 us -> 79.9 us (0.28)
  the two profiles are of different devices: /device:TPU:6 before, /device:TPU:16 now
where the time goes in v1:
time: 79.9 us; the launch traced here: 79.7 us
  Pallas kernels  72.8 us (91%)
  local copies, waits for them, and re-layouts  6.19 us (8%)
    pallas_call x1, Pallas kernels, shards(): pl.pallas_call(functools.partial(body, DN, C), out_shape=(jax.ShapeDtypeS...  72.8 us
    unnamed x12, local copies, waits for them, and re-layouts  6.19 us

profile of v1, /device:TPU:16, one launch (start us, length us, event | category | flops | bytes accessed | tf_op | source)
XLA Modules:
  0.0 79.7 jit_solution(13898724727490347423)
XLA Ops:
  0.6 0.0 copy-start
  0.6 1.0 %copy-done = bf16[1,64,64,32]{2,3,1,0:T(8,128)(2,1)S(1)} copy-done((bf16[1,64,64,32]{2,3,1,0:T(8,128)(2,1)S(1)}, bf16[1,64,64,32]{2,3,1,0:T(8,128)(2,1)}, u32[]{:S(2)}) %copy-start) | copy-done | bytes 262168
  1.7 0.0 copy-start.1
  1.7 0.9 %copy-done.1 = bf16[1,2,64,1024]{3,2,1,0:T(8,128)(2,1)S(1)} copy-done((bf16[1,2,64,1024]{3,2,1,0:T(8,128)(2,1)S(1)}, bf16[1,2,64,1024]{3,2,1,0:T(8,128)(2,1)}, u32[]{:S(2)}) %copy-start.1) | copy-done | bytes 262168
  2.6 0.0 copy-start.2
  2.6 0.9 %copy-done.2 = bf16[27,32,32]{2,1,0:T(8,128)(2,1)S(1)} copy-done((bf16[27,32,32]{2,1,0:T(8,128)(2,1)S(1)}, bf16[27,32,32]{2,1,0:T(8,128)(2,1)}, u32[]{:S(2)}) %copy-start.2) | copy-done | bytes 55320
  3.6 0.0 copy-start.3
  3.6 0.9 %copy-done.3 = bf16[64,1024]{1,0:T(8,128)(2,1)S(1)} copy-done((bf16[64,1024]{1,0:T(8,128)(2,1)S(1)}, bf16[64,1024]{1,0:T(8,128)(2,1)}, u32[]{:S(2)}) %copy-start.3) | copy-done | bytes 131096
  4.5 0.0 copy-start.4
  4.5 0.9 %copy-done.4 = bf16[64,1024]{1,0:T(8,128)(2,1)S(1)} copy-done((bf16[64,1024]{1,0:T(8,128)(2,1)S(1)}, bf16[64,1024]{1,0:T(8,128)(2,1)}, u32[]{:S(2)}) %copy-start.4) | copy-done | bytes 131096
  5.4 72.8 %shard_map.68 = (bf16[128,1024]{1,0:T(8,128)(2,1)S(1)}, f32[27,32,32]{2,1,0:T(8,128)S(1)}) custom-call(bf16[128,1024]{1,0:T(8,128)(2,1)S(1)} %bitcast.6, bf16[64,32,64]{2,1,0:T(8,128)(2,1)S(1)} %bitcast.5, bf16[64,1024]{1,0:T(8,128)(2,1)S(1)} %copy-done.3, bf16[64,1024]{1,0:T(8,128)(2,1)S(1)} %copy-done.4, bf16[27,32,32]{2,1,0:T(8,128)(2,1)S(1)} %copy-done.2), custom_call_target="tpu_custom_call" | custom-call | tf_op jit(solution)/shard_map/pallas_call | solution.py:426
  78.2 0.7 copy.9
  78.9 0.8 copy.10
Async XLA Ops:
  0.6 1.0 %copy-start = (bf16[1,64,64,32]{2,3,1,0:T(8,128)(2,1)S(1)}, bf16[1,64,64,32]{2,3,1,0:T(8,128)(2,1)}, u32[]{:S(2)}) copy-start(bf16[1,64,64,32]{2,3,1,0:T(8,128)(2,1)} %param.6) | copy-start | bytes 786436
  1.7 0.9 %copy-start.1 = (bf16[1,2,64,1024]{3,2,1,0:T(8,128)(2,1)S(1)}, bf16[1,2,64,1024]{3,2,1,0:T(8,128)(2,1)}, u32[]{:S(2)}) copy-start(bf16[1,2,64,1024]{3,2,1,0:T(8,128)(2,1)} %param.5) | copy-start | bytes 786436
  2.6 0.9 %copy-start.2 = (bf16[27,32,32]{2,1,0:T(8,128)(2,1)S(1)}, bf16[27,32,32]{2,1,0:T(8,128)(2,1)}, u32[]{:S(2)}) copy-start(bf16[27,32,32]{2,1,0:T(8,128)(2,1)} %kern_ref.1) | copy-start | bytes 165892
  3.6 0.9 %copy-start.3 = (bf16[64,1024]{1,0:T(8,128)(2,1)S(1)}, bf16[64,1024]{1,0:T(8,128)(2,1)}, u32[]{:S(2)}) copy-start(bf16[64,1024]{1,0:T(8,128)(2,1)} %wi_ref.1) | copy-start | bytes 393220
  4.5 0.9 %copy-start.4 = (bf16[64,1024]{1,0:T(8,128)(2,1)S(1)}, bf16[64,1024]{1,0:T(8,128)(2,1)}, u32[]{:S(2)}) copy-start(bf16[64,1024]{1,0:T(8,128)(2,1)} %wo_ref.1) | copy-start | bytes 393220

commit v2 on v1

v2 whole, which is shorter than its diff:
```python
import functools

import jax
import jax.numpy as jnp
from jax import lax
from jax.experimental import pallas as pl
from jax.experimental.pallas import tpu as pltpu
from jax.sharding import PartitionSpec as P

MESH = pl.DeviceIdType.MESH
BF = jnp.bfloat16
F32 = jnp.float32


def body(
    DN, C,
    go_hbm, pre_hbm, wi_hbm, wo_hbm, kern_hbm,
    out_hbm, kg_hbm,
    out_ref, kg_ref,
    pre_ref, wi_ref, wo_own, kern_ref, go_buf, wo_buf, wi_buf, wi_own, mt_buf, m_buf, xa, xb, pre2, kmf, kmat, acc, gp_stage, gpr,
    gbuf, g_stage, g_recv, g_fin, p_send, p_recv,
    in_sem, out_sem, go_sem, wo_s, wo_r, wi_s, wi_r, wi_rest, a1_s, a1_r, h_s, h_r, a2_s, a2_r, rs_s, rs_r, ag_s, ag_r, p_s, p_r,
):
    HN = 2 * DN
    Z = DN // 2
    NQ = HN // 4
    NCH = h_r.shape[1]
    KPC = DN // NCH
    SPD = g_stage.shape[1]
    NP = p_send.shape[0]
    PW = C // NP

    d = lax.axis_index("depth")
    h = lax.axis_index("height")
    k = h // 2
    c = h % 2
    xh = d // Z
    z = d % Z

    def remote(src, dst, ss, rs, dd, hh):
        return pltpu.make_async_remote_copy(
            src_ref=src, dst_ref=dst, send_sem=ss, recv_sem=rs, device_id=(dd, hh), device_id_type=MESH
        )

    partner = 2 * k + (1 - c)
    own_cells = pl.ds(pl.multiple_of(128 * c, 128), 128)
    loads = [
        pltpu.make_async_copy(go_hbm, go_buf.at[own_cells, :], in_sem.at[0]),
        pltpu.make_async_copy(wo_hbm.at[pl.ds(pl.multiple_of(32 * c, 32), 32), :], wo_own, in_sem.at[1]),
        pltpu.make_async_copy(kern_hbm, kern_ref, in_sem.at[2]),
        pltpu.make_async_copy(pre_hbm, pre_ref, in_sem.at[3]),
        pltpu.make_async_copy(wi_hbm, wi_ref, in_sem.at[4]),
    ]
    for load in loads:
        load.start()

    barrier = pltpu.get_barrier_semaphore()
    pl.semaphore_signal(barrier, inc=1, device_id=(d, partner), device_id_type=MESH)

    @pl.loop(1, DN)
    def _(j):
        pl.semaphore_signal(barrier, inc=1, device_id=((d + j) % DN, h), device_id_type=MESH)
        pl.semaphore_signal(barrier, inc=1, device_id=(d, 2 * ((k + j) % DN) + c), device_id_type=MESH)

    zero_tile = jnp.zeros((32, 128), BF)
    for s in range(3):
        m_buf[s, 0] = zero_tile
        m_buf[s, HN + 1] = zero_tile

    @pl.when(d == 0)
    def _():
        m_buf[2] = jnp.zeros(m_buf.shape[1:], BF)

    @pl.when(d == DN - 1)
    def _():
        m_buf[0] = jnp.zeros(m_buf.shape[1:], BF)

    for load in loads:
        load.wait()
    for o in range(27):
        s, m = divmod(o, 9)
        kmf[s, :, 32 * m : 32 * m + 32] = kern_ref[o].astype(F32)
    for s in range(3):
        kmat[s] = kmf[s].astype(BF)

    @pl.loop(0, HN)
    def _(t):
        both = jnp.concatenate([pre_ref[2 * t].astype(F32), pre_ref[2 * t + 1].astype(F32)], axis=1)
        pre2[t] = both.astype(BF)

    pl.semaphore_wait(barrier, 1 + 2 * (DN - 1))

    go_copy = remote(go_buf.at[own_cells, :], go_buf.at[own_cells, :], go_sem.at[0], go_sem.at[1], d, partner)
    go_copy.start()

    y = k % Z
    side = k - y
    near_y = (side + (y + 1) % Z, side + (y + Z - 1) % Z)
    held = y % 2

    class Ring:
        def __init__(self, own, buf, view, ss, rs, rest):
            self.own, self.buf, self.view, self.ss, self.rs, self.rest = own, buf, view, ss, rs, rest
            self.first = [(True, 0)]
            self.second = []
            for dz in (2, -2, 1, -1, 3, -3, 4, -4):
                for far in (False, True):
                    limit = Z // 2 if far == (dz < 0) else (Z - 1) // 2
                    if abs(dz) <= limit:
                        (self.first if abs(dz) <= 2 else self.second).append((far, dz))

        def copy(self, src, dst, sem, dd, hh):
            remote(src, dst, self.ss.at[0], sem, dd, hh).start()

        def idx(self, far, dz):
            return (1 - xh if far else xh) * Z + (z + dz + Z) % Z

        def held(self, i):
            return self.view(self.buf.at[i], 2 * held, 2)

        def begin(self):
            mine = self.view(self.own, 2 * held, 2)
            for far, dz in self.first[1:] + self.first[:1]:
                self.copy(mine, self.held(d), self.rs.at[0, d], self.idx(far, dz), h)

        def take(self, far, dz):
            i = self.idx(far, -dz)
            remote(self.held(i), self.held(i), self.ss.at[0], self.rs.at[0, i], d, partner).wait_recv()
            if abs(dz) == 2:
                for other, more in self.second:
                    if other == far and more * dz > 0:
                        self.copy(self.held(i), self.held(i), self.rs.at[0, i], self.idx(False, more - dz), h)

        def share(self, far, dz):
            i = self.idx(far, -dz)
            for e in range(2):
                part = self.view(self.buf.at[i], 2 * held + e, 1)
                self.copy(part, part, self.rest(i), d, 2 * near_y[e] + c)

        def complete(self, far, dz):
            i = self.idx(far, -dz)
            part = self.view(self.buf.at[i], 2 - 2 * held, 2)
            remote(part, part, self.ss.at[0], self.rest(i), d, partner).wait_recv()
            return i

        def finish(self):
            sent = self.buf.at[pl.ds(0, DN - 1)]
            remote(sent, sent, self.ss.at[0], self.rs.at[0, 0], d, partner).wait_send()

    def by_column(ref, first, n):
        return ref.at[:, pl.ds(pl.multiple_of(first * (C // 4), C // 4), n * (C // 4))]

    def by_row(ref, first, n):
        return ref.at[pl.ds(pl.multiple_of(first * 16, 16), n * 16), :]

    ring_o = Ring(wo_own, wo_buf, by_column, wo_s, wo_r, lambda i: wo_r.at[1, i])
    ring_i = Ring(wi_own, wi_buf, by_row, wi_s, wi_r, lambda i: wi_rest.at[0])
    ring_o.begin()

    col = lax.broadcasted_iota(jnp.int32, (C, C // 2), 1)
    row = lax.broadcasted_iota(jnp.int32, (C, C // 2), 0)
    pick = jnp.where(row == 64 * (col // 32) + 32 * c + col % 32, 1.0, 0.0).astype(BF)
    wi_own[...] = jnp.dot(wi_ref[...], pick, preferred_element_type=F32).astype(BF)

    def project(block, i):
        mid = lax.dot_general(block, go_buf[...], (((1,), (1,)), ((), ())), preferred_element_type=F32)
        mid = mid.astype(BF)

        @pl.when(i == k)
        def _():
            m_buf[1, 1 + 2 * i] = mid[:, :128]
            m_buf[1, 2 + 2 * i] = mid[:, 128:]

        @pl.when(i != k)
        def _():
            mt_buf[i, 0] = mid[:, :128]
            mt_buf[i, 1] = mid[:, 128:]
            remote(
                mt_buf.at[i], m_buf.at[1, pl.ds(1 + 2 * k, 2)], a1_s.at[0], a1_r.at[k // KPC], d, 2 * i + c
            ).start()

    go_copy.wait_recv()
    project(wo_own[...], d)
    waiting = []

    def next_block():
        if waiting:
            i = ring_o.complete(*waiting.pop(0))
            project(wo_buf[i], i)

    for far, dz in ring_o.first:
        ring_o.take(far, dz)
        ring_o.share(far, dz)
        waiting.append((far, dz))
        if len(waiting) > 5:
            next_block()
    ring_i.begin()
    for far, dz in ring_o.second:
        ring_o.take(far, dz)
        ring_o.share(far, dz)
        waiting.append((far, dz))
        next_block()
    while waiting:
        next_block()

    up, down = jnp.minimum(d + 1, DN - 1), jnp.maximum(d - 1, 0)

    def halo(n, side):
        part = pl.ds(1 + 2 * KPC * n, 2 * KPC)
        return remote(
            m_buf.at[1, part],
            m_buf.at[2 if side == 0 else 0, part],
            h_s.at[side],
            h_r.at[side, n],
            up if side == 0 else down,
            h,
        )

    for n in range(NCH):
        for there, tiles in ((n != k // KPC, 2 * KPC), (n == k // KPC, 2 * KPC - 2)):
            @pl.when(there)
            def _(n=n, tiles=tiles):
                part = m_buf.at[1, pl.ds(1, tiles)]
                remote(part, part, a1_s.at[0], a1_r.at[n], d, partner).wait_recv()

        @pl.when(d < DN - 1)
        def _(n=n):
            halo(n, 0).start()

        @pl.when(d > 0)
        def _(n=n):
            halo(n, 1).start()

    for far, dz in ring_i.first:
        ring_i.take(far, dz)

    lane = lax.broadcasted_iota(jnp.int32, (4, 32, 128), 2)
    low = lane < 64
    first = lane % 64 == 0
    last = lane % 64 == 63

    def widen(dst, s, at, n, v):
        v0 = v[:n]
        zero = jnp.zeros_like(v0)
        dst[s, pl.ds(at, n), 0:32, :] = jnp.where(last[:n], zero, pltpu.roll(v0, 127, 2)).astype(BF)
        dst[s, pl.ds(at, n), 32:64, :] = v0.astype(BF)
        dst[s, pl.ds(at, n), 64:96, :] = jnp.where(first[:n], zero, pltpu.roll(v0, 1, 2)).astype(BF)

    def spread(s, q):
        here = m_buf[s, pl.ds(1 + 4 * q, 4)].astype(F32)
        before = m_buf[s, pl.ds(4 * q, 4)].astype(F32)
        widen(xa, s, 4 * q, 4, here)
        widen(xb, s, 4 * q, 4, jnp.where(low, pltpu.roll(before, 64, 2), pltpu.roll(here, 64, 2)))

    def spread_next(s, t):
        before = m_buf[s, pl.ds(t, 1)].astype(F32)
        here = m_buf[s, pl.ds(t + 1, 1)].astype(F32)
        widen(xb, s, t, 1, jnp.where(low[:1], pltpu.roll(before, 64, 2), pltpu.roll(here, 64, 2)))

    def columns(s, q):
        tiles = []
        for j in range(4):
            t = 4 * q + j
            tiles.append(jnp.concatenate([xb[s, t + 1], xa[s, t], xb[s, t]], axis=0))
        return jnp.concatenate(tiles, axis=1)

    def hidden(q):
        tiles = [jnp.maximum(pre2[4 * q + j], jnp.zeros((32, 128), BF)) for j in range(4)]
        return jnp.concatenate(tiles, axis=1)

    def outer(x, q):
        return lax.dot_general(hidden(q), x, (((1,), (1,)), ((), ())), preferred_element_type=F32)

    gbuf[...] = jnp.zeros_like(gbuf)

    spread_next(1, HN)

    @pl.loop(0, NQ)
    def _(p):
        q = NQ - 1 - p
        spread(1, q)
        x = columns(1, q)
        acc[q] = jnp.dot(kmat[1], x, preferred_element_type=F32)
        gbuf[1, :, 0:288] += outer(x, q)

    for far, dz in ring_i.first:
        ring_i.share(far, dz)

    for n in range(NCH):
        @pl.when(d < DN - 1)
        def _(n=n):
            halo(n, 1).wait_recv()

        @pl.when(d > 0)
        def _(n=n):
            halo(n, 0).wait_recv()


    @pl.loop(0, NQ)
    def _(p):
        q = (p + k // 2) % NQ
        for s in (0, 2):
            spread(s, q)
            spread_next(s, 4 * q + 4)
        back = acc[q] + jnp.dot(kmat[0], columns(0, q), preferred_element_type=F32)
        back = back + jnp.dot(kmat[2], columns(2, q), preferred_element_type=F32)
        for j in range(4):
            gate = pre2[4 * q + j].astype(F32) > 0
            tile = jnp.where(gate, back[:, 128 * j : 128 * j + 128], jnp.zeros((32, 128), F32))
            gp_stage[4 * q + j] = tile.astype(BF)
        for j in range(2):
            i = 2 * q + j

            @pl.when(i == k)
            def _(i=i):
                for t in range(2):
                    gpr[t, pl.ds(pl.multiple_of(32 * k, 32), 32), :] = gp_stage[2 * i + t]

            @pl.when(i != k)
            def _(i=i):
                remote(
                    gp_stage.at[pl.ds(2 * i, 2)],
                    gpr.at[:, pl.ds(pl.multiple_of(32 * k, 32), 32), :],
                    a2_s.at[0],
                    a2_r.at[0],
                    d,
                    2 * i + c,
                ).start()

    for far, dz in ring_i.second:
        ring_i.take(far, dz)
        ring_i.share(far, dz)

    @pl.loop(0, NQ)
    def _(q):
        gbuf[0, :, 0:288] += outer(columns(0, q), q)
        gbuf[2, :, 0:288] += outer(columns(2, q), q)

    def slot(f):
        return f // SPD, f % SPD

    def cut(f):
        s, rest = divmod(f, 12)
        rb, lt = divmod(rest, 3)
        return s, slice(8 * rb, 8 * rb + 8), slice(128 * lt, 128 * lt + 128)

    for f in range(SPD * DN):
        a, b = slot(f)
        g_stage[a, b] = gbuf[cut(f)].astype(BF) if f < 36 else jnp.zeros((8, 128), BF)

    @pl.loop(1, DN)
    def _(j):
        r = (d + j) % DN
        remote(g_stage.at[r], g_recv.at[d], rs_s.at[0], rs_r.at[0], r, h).start()

    part = g_recv.at[pl.ds(0, DN - 1)]
    remote(part, part, rs_s.at[0], rs_r.at[0], d, partner).wait_recv()
    total = g_stage[d].astype(F32)
    for j in range(1, DN):
        r = (d + j) % DN
        total = total + g_recv[r].astype(F32)
    g_fin[d] = total.astype(BF)

    @pl.loop(1, DN)
    def _(j):
        r = (d + j) % DN
        remote(g_fin.at[d], g_fin.at[d], ag_s.at[0], ag_r.at[0], r, h).start()

    part = wi_buf.at[pl.ds(0, DN - 1), pl.ds(0, 32), :]
    remote(part, part, wi_s.at[0], wi_rest.at[0], d, partner).wait_recv()
    wi_buf[d] = wi_own[...]

    part = gpr.at[:, pl.ds(0, 32 * (DN - 1)), :]
    remote(part, part, a2_s.at[0], a2_r.at[0], d, partner).wait_recv()

    rows_p = wi_buf.shape[0] // NP

    def half(cells, n):
        w = wi_buf[rows_p * n : rows_p * (n + 1)].reshape(PW, C // 2)
        return lax.dot_general(cells, w, (((1,), (1,)), ((), ())), preferred_element_type=F32)

    theirs = gpr[1 - c].T
    exchange = []
    for n in range(NP):
        p_send[n] = half(theirs, n)
        copy = remote(p_send.at[n], p_recv.at[n], p_s.at[0], p_r.at[n], d, partner)
        copy.start()
        exchange.append(copy)

    mine = gpr[c].T
    for n in range(NP):
        part = half(mine, n)
        exchange[n].wait_recv()
        cols = slice(PW * n, PW * (n + 1))
        out_ref[:, cols] = (go_buf[own_cells, cols].astype(F32) + (part + p_recv[n])).astype(BF)
        pltpu.make_async_copy(out_ref.at[:, cols], out_hbm.at[:, cols], out_sem.at[0]).start()

    part = g_fin.at[pl.ds(0, DN - 1)]
    remote(part, part, ag_s.at[0], ag_r.at[0], d, partner).wait_recv()

    scale = float(DN * 2 * HN * 64) ** -0.5
    for f in range(36):
        gbuf[cut(f)] = g_fin[slot(f)].astype(F32) * scale
    for o in range(27):
        s, m = divmod(o, 9)
        kg_ref[o] = gbuf[s, :, 32 * m : 32 * m + 32]

    pltpu.make_async_copy(kg_ref, kg_hbm, out_sem.at[1]).start()

    go_copy.wait_send()
    ring_o.finish()
    ring_i.finish()

    def left(part, sem):
        remote(part, part, sem, go_sem.at[1], d, partner).wait_send()

    left(p_send, p_s.at[0])
    for side, there in ((0, d < DN - 1), (1, d > 0)):
        @pl.when(there)
        def _(side=side):
            left(m_buf.at[1, pl.ds(1, HN)], h_s.at[side])

    left(mt_buf.at[pl.ds(0, DN - 1)], a1_s.at[0])
    left(gp_stage.at[pl.ds(0, 2 * (DN - 1))], a2_s.at[0])
    left(g_stage.at[pl.ds(0, DN - 1)], rs_s.at[0])
    left(g_fin.at[pl.ds(0, DN - 1)], ag_s.at[0])
    pltpu.make_async_copy(out_ref, out_hbm, out_sem.at[0]).wait()
    pltpu.make_async_copy(kg_ref, kg_hbm, out_sem.at[1]).wait()


def shards(DN, grad_out, pre_act, w_in, w_out, kernel):
    C = grad_out.shape[-1]
    HN = 2 * DN
    rows = grad_out.reshape(128, C)
    turned = jnp.transpose(pre_act, (0, 1, 3, 2)).reshape(2 * HN, 32, 64)
    nch = max(1, DN // 4)
    spd = -(-36 // DN)
    np_ = max(1, C // 256)
    dma = pltpu.SemaphoreType.DMA
    grad_in, kernel_grad = pl.pallas_call(
        functools.partial(body, DN, C),
        out_shape=(
            jax.ShapeDtypeStruct((128, C), BF),
            jax.ShapeDtypeStruct((27, 32, 32), F32),
        ),
        in_specs=[pl.BlockSpec(memory_space=pltpu.HBM)] * 5,
        out_specs=(pl.BlockSpec(memory_space=pl.ANY),) * 2,
        scratch_shapes=[
            pltpu.VMEM((128, C), BF),
            pltpu.VMEM((27, 32, 32), F32),
            pltpu.VMEM((2 * HN, 32, 64), BF),
            pltpu.VMEM((64, C), BF),
            pltpu.VMEM((32, C), BF),
            pltpu.VMEM((27, 32, 32), BF),
            pltpu.VMEM((256, C), BF),
            pltpu.VMEM((DN, 32, C), BF),
            pltpu.VMEM((DN, 64, C // 2), BF),
            pltpu.VMEM((64, C // 2), BF),
            pltpu.VMEM((DN, 2, 32, 128), BF),
            pltpu.VMEM((3, HN + 2, 32, 128), BF),
            pltpu.VMEM((3, HN, 96, 128), BF),
            pltpu.VMEM((3, HN + 1, 96, 128), BF),
            pltpu.VMEM((HN, 32, 128), BF),
            pltpu.VMEM((3, 32, 288), F32),
            pltpu.VMEM((3, 32, 288), BF),
            pltpu.VMEM((HN // 4, 32, 512), F32),
            pltpu.VMEM((HN, 32, 128), BF),
            pltpu.VMEM((2, C // 2, 128), BF),
            pltpu.VMEM((3, 32, 384), F32),
            pltpu.VMEM((DN, spd, 8, 128), BF),
            pltpu.VMEM((DN, spd, 8, 128), BF),
            pltpu.VMEM((DN, spd, 8, 128), BF),
            pltpu.VMEM((np_, 128, C // np_), F32),
            pltpu.VMEM((np_, 128, C // np_), F32),
            dma((5,)),
            dma((2,)),
            dma((2,)),
            dma((1,)),
            dma((2, DN)),
            dma((1,)),
            dma((1, DN)),
            dma((1,)),
            dma((1,)),
            dma((nch,)),
            dma((2,)),
            dma((2, nch)),
            dma((1,)),
            dma((1,)),
            dma((1,)),
            dma((1,)),
            dma((1,)),
            dma((1,)),
            dma((1,)),
            dma((np_,)),
        ],
        compiler_params=pltpu.CompilerParams(
            collective_id=0, has_side_effects=True, vmem_limit_bytes=63 << 20
        ),
    )(rows, turned, w_in, w_out, kernel)
    return grad_in.reshape(grad_out.shape), kernel_grad


def solution(mesh):
    in_specs = (
        P("depth", "height", None, None),
        P("depth", None, None, "height"),
        P("depth", None),
        P("depth", None),
        P(None, None, "height"),
    )
    out_specs = (P("depth", "height", None, None), P(None, None, "height"))
    step = functools.partial(shards, mesh.shape["depth"])
    return jax.shard_map(step, mesh=mesh, in_specs=in_specs, out_specs=out_specs, check_vma=False)
```

time: 79.9 us -> 69.3 us (0.87)
  the two profiles are of different devices: /device:TPU:16 before, /device:TPU:1 now
where the time goes in v2:
time: 69.3 us; the launch traced here: 68.2 us
  Pallas kernels  65.1 us (94%)
  local copies, waits for them, and re-layouts  2.49 us (4%)
    pallas_call x1, Pallas kernels, shards(): pl.pallas_call(functools.partial(body, DN, C), out_shape=(jax.ShapeDtypeS...  65.1 us
    unnamed x4, local copies, waits for them, and re-layouts  2.49 us

profile of v2, /device:TPU:1, one launch (start us, length us, event | category | flops | bytes accessed | tf_op | source)
XLA Modules:
  0.0 68.2 jit_solution(7707103031266439503)
XLA Ops:
  0.6 65.1 %shard_map.68 = (bf16[128,1024]{1,0:T(8,128)(2,1)}, f32[27,32,32]{2,1,0:T(8,128)}) custom-call(bf16[128,1024]{1,0:T(8,128)(2,1)} %bitcast.6, bf16[64,32,64]{2,1,0:T(8,128)(2,1)} %bitcast.5, bf16[64,1024]{1,0:T(8,128)(2,1)} %wi_hbm.1, bf16[64,1024]{1,0:T(8,128)(2,1)} %wo_hbm.1, bf16[27,32,32]{2,1,0:T(8,128)(2,1)} %kern_hbm.1), custom_call_target="tpu_custom_call" | custom-call | tf_op jit(solution)/shard_map/pallas_call | solution.py:440
  65.7 0.0 copy-start
  65.7 1.7 %copy.9 = bf16[1,2,64,1024]{3,2,1,0:T(8,128)(2,1)} copy(bf16[1,2,64,1024]{3,2,1,0:T(8,128)(2,1)} %bitcast.7) | data formatting | bytes 524288
  67.4 0.0 copy-done
  67.4 0.8 %copy.10 = f32[27,32,32]{2,1,0:T(8,128)} copy(f32[27,32,32]{2,1,0:T(8,128)S(1)} %copy-done) | data formatting | bytes 221184
Async XLA Ops:
  65.7 1.7 %copy-start = (f32[27,32,32]{2,1,0:T(8,128)S(1)}, f32[27,32,32]{2,1,0:T(8,128)}, u32[]{:S(2)}) copy-start(f32[27,32,32]{2,1,0:T(8,128)} %get-tuple-element.9) | copy-start | bytes 331780

commit v3 on v2

--- a/solution.py
+++ b/solution.py
@@ -19,7 +19,7 @@
     out_ref, kg_ref,
     pre_ref, wi_ref, wo_own, kern_ref, go_buf, wo_buf, wi_buf, wi_own, mt_buf, m_buf, xa, xb, pre2, kmf, kmat, acc, gp_stage, gpr,
     gbuf, g_stage, g_recv, g_fin, p_send, p_recv,
-    in_sem, out_sem, go_sem, wo_s, wo_r, wi_s, wi_r, wi_rest, a1_s, a1_r, h_s, h_r, a2_s, a2_r, rs_s, rs_r, ag_s, ag_r, p_s, p_r,
+    in_sem, out_sem, go_sem, gx_s, gx_r, gf_s, gf_r, wo_s, wo_r, wi_s, wi_r, wi_rest, a1_s, a1_r, h_s, h_r, a2_s, a2_r, rs_s, rs_r, ag_s, ag_r, p_s, p_r,
 ):
     HN = 2 * DN
     Z = DN // 2
@@ -42,7 +42,10 @@
             src_ref=src, dst_ref=dst, send_sem=ss, recv_sem=rs, device_id=(dd, hh), device_id_type=MESH
         )
 
+    xl = k // Z
+    y = k % Z
     partner = 2 * k + (1 - c)
+    pair = (k + Z) % DN
     own_cells = pl.ds(pl.multiple_of(128 * c, 128), 128)
     loads = [
         pltpu.make_async_copy(go_hbm, go_buf.at[own_cells, :], in_sem.at[0]),
@@ -62,6 +65,17 @@
         pl.semaphore_signal(barrier, inc=1, device_id=((d + j) % DN, h), device_id_type=MESH)
         pl.semaphore_signal(barrier, inc=1, device_id=(d, 2 * ((k + j) % DN) + c), device_id_type=MESH)
 
+    steps = [dz for dz in (2, -2, 1, -1) if (abs(dz) <= Z // 2 if dz > 0 else abs(dz) <= (Z - 1) // 2)]
+    across = xh != xl
+
+    def served(dz):
+        return xl * Z + (z + dz + Z) % Z, 2 * (xh * Z + y) + c
+
+    @pl.when(across)
+    def _():
+        for dz in steps + [0]:
+            pl.semaphore_signal(barrier, inc=1, device_id=served(dz), device_id_type=MESH)
+
     zero_tile = jnp.zeros((32, 128), BF)
     for s in range(3):
         m_buf[s, 0] = zero_tile
@@ -88,12 +102,22 @@
         both = jnp.concatenate([pre_ref[2 * t].astype(F32), pre_ref[2 * t + 1].astype(F32)], axis=1)
         pre2[t] = both.astype(BF)
 
-    pl.semaphore_wait(barrier, 1 + 2 * (DN - 1))
+    pl.semaphore_wait(barrier, 1 + 2 * (DN - 1) + jnp.where(across, len(steps) + 1, 0))
 
     go_copy = remote(go_buf.at[own_cells, :], go_buf.at[own_cells, :], go_sem.at[0], go_sem.at[1], d, partner)
     go_copy.start()
 
-    y = k % Z
+    NF = gx_r.shape[0]
+
+    def cells(first, n):
+        return go_buf.at[pl.ds(pl.multiple_of(first + 128 * c + 128 // NF * n, 128 // NF), 128 // NF), :]
+
+    far_go = [remote(cells(0, n), cells(256, n), gx_s.at[0], gx_r.at[n], d, 2 * pair + c) for n in range(NF)]
+
+    def pass_cells(n):
+        far_go[n].wait_recv()
+        remote(cells(256, n), cells(256, n), gf_s.at[0], gf_r.at[0], d, partner).start()
+
     side = k - y
     near_y = (side + (y + 1) % Z, side + (y + Z - 1) % Z)
     held = y % 2
@@ -147,61 +171,89 @@
             sent = self.buf.at[pl.ds(0, DN - 1)]
             remote(sent, sent, self.ss.at[0], self.rs.at[0, 0], d, partner).wait_send()
 
-    def by_column(ref, first, n):
-        return ref.at[:, pl.ds(pl.multiple_of(first * (C // 4), C // 4), n * (C // 4))]
-
     def by_row(ref, first, n):
         return ref.at[pl.ds(pl.multiple_of(first * 16, 16), n * 16), :]
 
-    ring_o = Ring(wo_own, wo_buf, by_column, wo_s, wo_r, lambda i: wo_r.at[1, i])
+
+    def send_block(src, dst, i, to):
+        remote(src, dst, wo_s.at[0], wo_r.at[i], *to).start()
+
+    for dz in steps:
+        send_block(wo_own, wo_buf.at[z], z, served(dz))
+
+    @pl.when(across)
+    def _():
+        send_block(wo_own, wo_buf.at[z], z, served(0))
+
+    @pl.when(xh == xl)
+    def _():
+        wo_buf[z] = wo_own[...]
+
+    for copy in far_go:
+        copy.start()
+
+    def take_block(dz):
+        i = (z - dz + Z) % Z
+        whole = wo_buf.at[i]
+        remote(whole, whole, wo_s.at[0], wo_r.at[i], d, partner).wait_recv()
+        if abs(dz) == 2 and Z >= 8:
+            on = dz // 2
+            half = whole.at[pl.ds(0 if dz > 0 else 16, 16), :]
+            send_block(whole, whole, i, (xh * Z + (z + on + Z) % Z, h))
+            send_block(half, half, i, (xh * Z + (z + dz + Z) % Z, h))
+        return i
+
     ring_i = Ring(wi_own, wi_buf, by_row, wi_s, wi_r, lambda i: wi_rest.at[0])
-    ring_o.begin()
-
     col = lax.broadcasted_iota(jnp.int32, (C, C // 2), 1)
     row = lax.broadcasted_iota(jnp.int32, (C, C // 2), 0)
     pick = jnp.where(row == 64 * (col // 32) + 32 * c + col % 32, 1.0, 0.0).astype(BF)
     wi_own[...] = jnp.dot(wi_ref[...], pick, preferred_element_type=F32).astype(BF)
 
-    def project(block, i):
-        mid = lax.dot_general(block, go_buf[...], (((1,), (1,)), ((), ())), preferred_element_type=F32)
-        mid = mid.astype(BF)
-
-        @pl.when(i == k)
-        def _():
-            m_buf[1, 1 + 2 * i] = mid[:, :128]
-            m_buf[1, 2 + 2 * i] = mid[:, 128:]
-
-        @pl.when(i != k)
-        def _():
-            mt_buf[i, 0] = mid[:, :128]
-            mt_buf[i, 1] = mid[:, 128:]
-            remote(
-                mt_buf.at[i], m_buf.at[1, pl.ds(1 + 2 * k, 2)], a1_s.at[0], a1_r.at[k // KPC], d, 2 * i + c
-            ).start()
+    def project(rows, blocks, side):
+        mids = lax.dot_general(
+            rows, go_buf[256 * side : 256 * side + 256], (((1,), (1,)), ((), ())), preferred_element_type=F32
+        ).astype(BF)
+        whose = pair if side else k
+        part = pl.ds(1 + 2 * whose, 2)
+        for n, i in enumerate(blocks):
+            mid = mids[32 * n : 32 * n + 32]
+
+            @pl.when(i == y)
+            def _(i=i, mid=mid):
+                m_buf[1, 1 + 2 * whose] = mid[:, :128]
+                m_buf[1, 2 + 2 * whose] = mid[:, 128:]
+
+            @pl.when(i != y)
+            def _(i=i, mid=mid):
+                at = 2 * i + side
+                mt_buf[at, 0] = mid[:, :128]
+                mt_buf[at, 1] = mid[:, 128:]
+                owner = 2 * (xl * Z + i) + c
+                remote(mt_buf.at[at], m_buf.at[1, part], a1_s.at[0], a1_r.at[whose // KPC], d, owner).start()
+
+    def stack(blocks):
+        return jnp.concatenate([wo_buf[i] for i in blocks], axis=0)
 
     go_copy.wait_recv()
-    project(wo_own[...], d)
-    waiting = []
-
-    def next_block():
-        if waiting:
-            i = ring_o.complete(*waiting.pop(0))
-            project(wo_buf[i], i)
-
-    for far, dz in ring_o.first:
-        ring_o.take(far, dz)
-        ring_o.share(far, dz)
-        waiting.append((far, dz))
-        if len(waiting) > 5:
-            next_block()
+    near = [take_block(dz) for dz in steps]
+    pass_cells(0)
+    pass_cells(1)
+
+    @pl.when(across)
+    def _():
+        take_block(0)
+
+    near.append(z)
+    project(stack(near), near, 0)
+    for n in range(2, NF):
+        pass_cells(n)
+    distant = [take_block(dz) for dz in (3, -3, 4)] if Z >= 8 else []
     ring_i.begin()
-    for far, dz in ring_o.second:
-        ring_o.take(far, dz)
-        ring_o.share(far, dz)
-        waiting.append((far, dz))
-        next_block()
-    while waiting:
-        next_block()
+    if distant:
+        project(stack(distant), distant, 0)
+    handed = go_buf.at[pl.ds(0, 128), :]
+    remote(handed, handed, gf_s.at[0], gf_r.at[0], d, partner).wait_recv()
+    project(wo_buf[...].reshape(32 * Z, C), list(range(Z)), 1)
 
     up, down = jnp.minimum(d + 1, DN - 1), jnp.maximum(d - 1, 0)
 
@@ -216,12 +268,11 @@
             h,
         )
 
-    for n in range(NCH):
-        for there, tiles in ((n != k // KPC, 2 * KPC), (n == k // KPC, 2 * KPC - 2)):
-            @pl.when(there)
-            def _(n=n, tiles=tiles):
-                part = m_buf.at[1, pl.ds(1, tiles)]
-                remote(part, part, a1_s.at[0], a1_r.at[n], d, partner).wait_recv()
+    turn = [(k // KPC + j) % NCH for j in range(NCH)]
+    for j, n in enumerate(turn):
+        tiles = 2 * KPC - 2 * (j == 0) - 2 * (j == NCH // 2)
+        part = m_buf.at[1, pl.ds(1, tiles)]
+        remote(part, part, a1_s.at[0], a1_r.at[n], d, partner).wait_recv()
 
         @pl.when(d < DN - 1)
         def _(n=n):
@@ -286,24 +337,15 @@
     for far, dz in ring_i.first:
         ring_i.share(far, dz)
 
-    for n in range(NCH):
-        @pl.when(d < DN - 1)
-        def _(n=n):
-            halo(n, 1).wait_recv()
-
-        @pl.when(d > 0)
-        def _(n=n):
-            halo(n, 0).wait_recv()
-
-
-    @pl.loop(0, NQ)
-    def _(p):
-        q = (p + k // 2) % NQ
+    def finish_quad(q):
         for s in (0, 2):
             spread(s, q)
             spread_next(s, 4 * q + 4)
-        back = acc[q] + jnp.dot(kmat[0], columns(0, q), preferred_element_type=F32)
-        back = back + jnp.dot(kmat[2], columns(2, q), preferred_element_type=F32)
+        back = acc[q]
+        for s in (0, 2):
+            x = columns(s, q)
+            back = back + jnp.dot(kmat[s], x, preferred_element_type=F32)
+            gbuf[s, :, 0:288] += outer(x, q)
         for j in range(4):
             gate = pre2[4 * q + j].astype(F32) > 0
             tile = jnp.where(gate, back[:, 128 * j : 128 * j + 128], jnp.zeros((32, 128), F32))
@@ -327,14 +369,22 @@
                     2 * i + c,
                 ).start()
 
-    for far, dz in ring_i.second:
-        ring_i.take(far, dz)
-        ring_i.share(far, dz)
-
-    @pl.loop(0, NQ)
-    def _(q):
-        gbuf[0, :, 0:288] += outer(columns(0, q), q)
-        gbuf[2, :, 0:288] += outer(columns(2, q), q)
+    done = 0
+    for j, n in enumerate(turn):
+        @pl.when(d < DN - 1)
+        def _(n=n):
+            halo(n, 1).wait_recv()
+
+        @pl.when(d > 0)
+        def _(n=n):
+            halo(n, 0).wait_recv()
+
+        ready = NQ if j == NCH - 1 else j * (NQ // NCH)
+        if ready > done:
+            @pl.loop(done, ready)
+            def _(p):
+                finish_quad((turn[0] * (NQ // NCH) + 1 + p) % NQ)
+        done = ready
 
     def slot(f):
         return f // SPD, f % SPD
@@ -352,6 +402,10 @@
     def _(j):
         r = (d + j) % DN
         remote(g_stage.at[r], g_recv.at[d], rs_s.at[0], rs_r.at[0], r, h).start()
+
+    for far, dz in ring_i.second:
+        ring_i.take(far, dz)
+        ring_i.share(far, dz)
 
     part = g_recv.at[pl.ds(0, DN - 1)]
     remote(part, part, rs_s.at[0], rs_r.at[0], d, partner).wait_recv()
@@ -408,7 +462,12 @@
     pltpu.make_async_copy(kg_ref, kg_hbm, out_sem.at[1]).start()
 
     go_copy.wait_send()
-    ring_o.finish()
+    for there, blocks in ((xh == xl, Z - 1), (across, Z)):
+        @pl.when(there)
+        def _(blocks=blocks):
+            sent = wo_buf.at[pl.ds(0, blocks)]
+            remote(sent, sent, wo_s.at[0], wo_r.at[0], d, partner).wait_send()
+
     ring_i.finish()
 
     def left(part, sem):
@@ -420,7 +479,9 @@
         def _(side=side):
             left(m_buf.at[1, pl.ds(1, HN)], h_s.at[side])
 
-    left(mt_buf.at[pl.ds(0, DN - 1)], a1_s.at[0])
+    left(mt_buf.at[pl.ds(0, DN - 2)], a1_s.at[0])
+    left(go_buf.at[pl.ds(0, 128), :], gx_s.at[0])
+    left(go_buf.at[pl.ds(0, 128), :], gf_s.at[0])
     left(gp_stage.at[pl.ds(0, 2 * (DN - 1))], a2_s.at[0])
     left(g_stage.at[pl.ds(0, DN - 1)], rs_s.at[0])
     left(g_fin.at[pl.ds(0, DN - 1)], ag_s.at[0])
@@ -452,8 +513,8 @@
             pltpu.VMEM((64, C), BF),
             pltpu.VMEM((32, C), BF),
             pltpu.VMEM((27, 32, 32), BF),
-            pltpu.VMEM((256, C), BF),
-            pltpu.VMEM((DN, 32, C), BF),
+            pltpu.VMEM((512, C), BF),
+            pltpu.VMEM((DN // 2, 32, C), BF),
             pltpu.VMEM((DN, 64, C // 2), BF),
             pltpu.VMEM((64, C // 2), BF),
             pltpu.VMEM((DN, 2, 32, 128), BF),
@@ -476,7 +537,11 @@
             dma((2,)),
             dma((2,)),
             dma((1,)),
-            dma((2, DN)),
+            dma((4,)),
+            dma((1,)),
+            dma((1,)),
+            dma((1,)),
+            dma((DN // 2,)),
             dma((1,)),
             dma((1, DN)),
             dma((1,)),

time: 69.3 us -> 62.2 us (0.90)
  the two profiles are of different devices: /device:TPU:1 before, /device:TPU:2 now
where the time goes in v3:
time: 62.2 us; the launch traced here: 62 us
  Pallas kernels  58.9 us (95%)
  local copies, waits for them, and re-layouts  2.49 us (4%)
  between operations  0.65 us (1%)
    pallas_call x1, Pallas kernels, shards(): pl.pallas_call(functools.partial(body, DN, C), out_shape=(jax.ShapeDtypeS...  58.9 us
    unnamed x4, local copies, waits for them, and re-layouts  2.49 us

profile of v3, /device:TPU:2, one launch (start us, length us, event | category | flops | bytes accessed | tf_op | source)
XLA Modules:
  0.0 62.0 jit_solution(13615876391658037829)
XLA Ops:
  0.6 58.9 %shard_map.68 = (bf16[128,1024]{1,0:T(8,128)(2,1)}, f32[27,32,32]{2,1,0:T(8,128)}) custom-call(bf16[128,1024]{1,0:T(8,128)(2,1)} %bitcast.6, bf16[64,32,64]{2,1,0:T(8,128)(2,1)} %bitcast.5, bf16[64,1024]{1,0:T(8,128)(2,1)} %wi_hbm.1, bf16[64,1024]{1,0:T(8,128)(2,1)} %wo_hbm.1, bf16[27,32,32]{2,1,0:T(8,128)(2,1)} %kern_hbm.1), custom_call_target="tpu_custom_call" | custom-call | tf_op jit(solution)/shard_map/pallas_call | solution.py:501
  59.5 0.0 copy-start
  59.5 1.7 %copy.9 = bf16[1,2,64,1024]{3,2,1,0:T(8,128)(2,1)} copy(bf16[1,2,64,1024]{3,2,1,0:T(8,128)(2,1)} %bitcast.7) | data formatting | bytes 524288
  61.2 0.0 copy-done
  61.3 0.8 %copy.10 = f32[27,32,32]{2,1,0:T(8,128)} copy(f32[27,32,32]{2,1,0:T(8,128)S(1)} %copy-done) | data formatting | bytes 221184
Async XLA Ops:
  59.5 1.7 %copy-start = (f32[27,32,32]{2,1,0:T(8,128)S(1)}, f32[27,32,32]{2,1,0:T(8,128)}, u32[]{:S(2)}) copy-start(f32[27,32,32]{2,1,0:T(8,128)} %get-tuple-element.9) | copy-start | bytes 331780

commit v4 on v3

--- a/solution.py
+++ b/solution.py
@@ -17,7 +17,7 @@
     go_hbm, pre_hbm, wi_hbm, wo_hbm, kern_hbm,
     out_hbm, kg_hbm,
     out_ref, kg_ref,
-    pre_ref, wi_ref, wo_own, kern_ref, go_buf, wo_buf, wi_buf, wi_own, mt_buf, m_buf, xa, xb, pre2, kmf, kmat, acc, gp_stage, gpr,
+    pre_ref, wi_ref, wo_own, kern_ref, go_buf, wo_buf, wi_buf, wi_own, mt_buf, m_buf, pre2, kmf, kmat, acc, gp_stage, gpr,
     gbuf, g_stage, g_recv, g_fin, p_send, p_recv,
     in_sem, out_sem, go_sem, gx_s, gx_r, gf_s, gf_r, wo_s, wo_r, wi_s, wi_r, wi_rest, a1_s, a1_r, h_s, h_r, a2_s, a2_r, rs_s, rs_r, ag_s, ag_r, p_s, p_r,
 ):
@@ -76,32 +76,8 @@
         for dz in steps + [0]:
             pl.semaphore_signal(barrier, inc=1, device_id=served(dz), device_id_type=MESH)
 
-    zero_tile = jnp.zeros((32, 128), BF)
-    for s in range(3):
-        m_buf[s, 0] = zero_tile
-        m_buf[s, HN + 1] = zero_tile
-
-    @pl.when(d == 0)
-    def _():
-        m_buf[2] = jnp.zeros(m_buf.shape[1:], BF)
-
-    @pl.when(d == DN - 1)
-    def _():
-        m_buf[0] = jnp.zeros(m_buf.shape[1:], BF)
-
-    for load in loads:
-        load.wait()
-    for o in range(27):
-        s, m = divmod(o, 9)
-        kmf[s, :, 32 * m : 32 * m + 32] = kern_ref[o].astype(F32)
-    for s in range(3):
-        kmat[s] = kmf[s].astype(BF)
-
-    @pl.loop(0, HN)
-    def _(t):
-        both = jnp.concatenate([pre_ref[2 * t].astype(F32), pre_ref[2 * t + 1].astype(F32)], axis=1)
-        pre2[t] = both.astype(BF)
-
+    loads[0].wait()
+    loads[1].wait()
     pl.semaphore_wait(barrier, 1 + 2 * (DN - 1) + jnp.where(across, len(steps) + 1, 0))
 
     go_copy = remote(go_buf.at[own_cells, :], go_buf.at[own_cells, :], go_sem.at[0], go_sem.at[1], d, partner)
@@ -204,11 +180,6 @@
         return i
 
     ring_i = Ring(wi_own, wi_buf, by_row, wi_s, wi_r, lambda i: wi_rest.at[0])
-    col = lax.broadcasted_iota(jnp.int32, (C, C // 2), 1)
-    row = lax.broadcasted_iota(jnp.int32, (C, C // 2), 0)
-    pick = jnp.where(row == 64 * (col // 32) + 32 * c + col % 32, 1.0, 0.0).astype(BF)
-    wi_own[...] = jnp.dot(wi_ref[...], pick, preferred_element_type=F32).astype(BF)
-
     def project(rows, blocks, side):
         mids = lax.dot_general(
             rows, go_buf[256 * side : 256 * side + 256], (((1,), (1,)), ((), ())), preferred_element_type=F32
@@ -234,7 +205,37 @@
     def stack(blocks):
         return jnp.concatenate([wo_buf[i] for i in blocks], axis=0)
 
-    go_copy.wait_recv()
+    for load in loads[2:]:
+        load.wait()
+    zero_tile = jnp.zeros((32, 128), BF)
+    for s in range(3):
+        m_buf[s, 0] = zero_tile
+        m_buf[s, HN + 1] = zero_tile
+
+    @pl.when(d == 0)
+    def _():
+        m_buf[2] = jnp.zeros(m_buf.shape[1:], BF)
+
+    @pl.when(d == DN - 1)
+    def _():
+        m_buf[0] = jnp.zeros(m_buf.shape[1:], BF)
+
+    for o in range(27):
+        s, m = divmod(o, 9)
+        kmf[s, :, 32 * m : 32 * m + 32] = kern_ref[o].astype(F32)
+    for s in range(3):
+        kmat[s] = kmf[s].astype(BF)
+
+    @pl.loop(0, HN)
+    def _(t):
+        both = jnp.concatenate([pre_ref[2 * t].astype(F32), pre_ref[2 * t + 1].astype(F32)], axis=1)
+        pre2[t] = both.astype(BF)
+
+    col = lax.broadcasted_iota(jnp.int32, (C, C // 2), 1)
+    row = lax.broadcasted_iota(jnp.int32, (C, C // 2), 0)
+    pick = jnp.where(row == 64 * (col // 32) + 32 * c + col % 32, 1.0, 0.0).astype(BF)
+    wi_own[...] = jnp.dot(wi_ref[...], pick, preferred_element_type=F32).astype(BF)
+
     near = [take_block(dz) for dz in steps]
     pass_cells(0)
     pass_cells(1)
@@ -244,17 +245,19 @@
         take_block(0)
 
     near.append(z)
+    go_copy.wait_recv()
     project(stack(near), near, 0)
     for n in range(2, NF):
         pass_cells(n)
-    distant = [take_block(dz) for dz in (3, -3, 4)] if Z >= 8 else []
-    ring_i.begin()
-    if distant:
-        project(stack(distant), distant, 0)
     handed = go_buf.at[pl.ds(0, 128), :]
     remote(handed, handed, gf_s.at[0], gf_r.at[0], d, partner).wait_recv()
-    project(wo_buf[...].reshape(32 * Z, C), list(range(Z)), 1)
-
+    project(stack(near), near, 1)
+    ring_i.begin()
+    if Z >= 8:
+        distant = [take_block(dz) for dz in (3, -3, 4)]
+        rows = stack(distant)
+        project(rows, distant, 0)
+        project(rows, distant, 1)
     up, down = jnp.minimum(d + 1, DN - 1), jnp.maximum(d - 1, 0)
 
     def halo(n, side):
@@ -282,38 +285,28 @@
         def _(n=n):
             halo(n, 1).start()
 
-    for far, dz in ring_i.first:
-        ring_i.take(far, dz)
-
-    lane = lax.broadcasted_iota(jnp.int32, (4, 32, 128), 2)
+    lane = lax.broadcasted_iota(jnp.int32, (5, 32, 128), 2)
     low = lane < 64
     first = lane % 64 == 0
     last = lane % 64 == 63
 
-    def widen(dst, s, at, n, v):
-        v0 = v[:n]
-        zero = jnp.zeros_like(v0)
-        dst[s, pl.ds(at, n), 0:32, :] = jnp.where(last[:n], zero, pltpu.roll(v0, 127, 2)).astype(BF)
-        dst[s, pl.ds(at, n), 32:64, :] = v0.astype(BF)
-        dst[s, pl.ds(at, n), 64:96, :] = jnp.where(first[:n], zero, pltpu.roll(v0, 1, 2)).astype(BF)
-
-    def spread(s, q):
-        here = m_buf[s, pl.ds(1 + 4 * q, 4)].astype(F32)
-        before = m_buf[s, pl.ds(4 * q, 4)].astype(F32)
-        widen(xa, s, 4 * q, 4, here)
-        widen(xb, s, 4 * q, 4, jnp.where(low, pltpu.roll(before, 64, 2), pltpu.roll(here, 64, 2)))
-
-    def spread_next(s, t):
-        before = m_buf[s, pl.ds(t, 1)].astype(F32)
-        here = m_buf[s, pl.ds(t + 1, 1)].astype(F32)
-        widen(xb, s, t, 1, jnp.where(low[:1], pltpu.roll(before, 64, 2), pltpu.roll(here, 64, 2)))
+    def shifts(v):
+        n = v.shape[0]
+        zero = jnp.zeros_like(v)
+        later = jnp.where(last[:n], zero, pltpu.roll(v, 127, 2))
+        sooner = jnp.where(first[:n], zero, pltpu.roll(v, 1, 2))
+        return later, v, sooner
 
     def columns(s, q):
-        tiles = []
+        tiles = m_buf[s, pl.ds(4 * q, 6)]
+        half = pltpu.roll(tiles, 64, 2)
+        even = shifts(tiles[1:5])
+        odd = shifts(jnp.where(low, half[0:5], half[1:6]))
+        parts = []
         for j in range(4):
-            t = 4 * q + j
-            tiles.append(jnp.concatenate([xb[s, t + 1], xa[s, t], xb[s, t]], axis=0))
-        return jnp.concatenate(tiles, axis=1)
+            column = [v[j + 1] for v in odd] + [v[j] for v in even] + [v[j] for v in odd]
+            parts.append(jnp.concatenate(column, axis=0))
+        return jnp.concatenate(parts, axis=1)
 
     def hidden(q):
         tiles = [jnp.maximum(pre2[4 * q + j], jnp.zeros((32, 128), BF)) for j in range(4)]
@@ -324,50 +317,42 @@
 
     gbuf[...] = jnp.zeros_like(gbuf)
 
-    spread_next(1, HN)
-
-    @pl.loop(0, NQ)
-    def _(p):
-        q = NQ - 1 - p
-        spread(1, q)
+    @pl.loop(0, NQ, unroll=min(NQ, 8))
+    def _(q):
         x = columns(1, q)
         acc[q] = jnp.dot(kmat[1], x, preferred_element_type=F32)
         gbuf[1, :, 0:288] += outer(x, q)
 
-    for far, dz in ring_i.first:
-        ring_i.share(far, dz)
-
-    def finish_quad(q):
-        for s in (0, 2):
-            spread(s, q)
-            spread_next(s, 4 * q + 4)
-        back = acc[q]
-        for s in (0, 2):
-            x = columns(s, q)
-            back = back + jnp.dot(kmat[s], x, preferred_element_type=F32)
-            gbuf[s, :, 0:288] += outer(x, q)
-        for j in range(4):
-            gate = pre2[4 * q + j].astype(F32) > 0
-            tile = jnp.where(gate, back[:, 128 * j : 128 * j + 128], jnp.zeros((32, 128), F32))
-            gp_stage[4 * q + j] = tile.astype(BF)
-        for j in range(2):
-            i = 2 * q + j
-
-            @pl.when(i == k)
-            def _(i=i):
-                for t in range(2):
-                    gpr[t, pl.ds(pl.multiple_of(32 * k, 32), 32), :] = gp_stage[2 * i + t]
-
-            @pl.when(i != k)
-            def _(i=i):
-                remote(
-                    gp_stage.at[pl.ds(2 * i, 2)],
-                    gpr.at[:, pl.ds(pl.multiple_of(32 * k, 32), 32), :],
-                    a2_s.at[0],
-                    a2_r.at[0],
-                    d,
-                    2 * i + c,
-                ).start()
+    def finish_quads(quads):
+        for q in quads:
+            back = acc[q]
+            for s in (0, 2):
+                x = columns(s, q)
+                back = back + jnp.dot(kmat[s], x, preferred_element_type=F32)
+                gbuf[s, :, 0:288] += outer(x, q)
+            for j in range(4):
+                gate = pre2[4 * q + j].astype(F32) > 0
+                tile = jnp.where(gate, back[:, 128 * j : 128 * j + 128], jnp.zeros((32, 128), F32))
+                gp_stage[4 * q + j] = tile.astype(BF)
+        for q in quads:
+            for j in range(2):
+                i = 2 * q + j
+
+                @pl.when(i == k)
+                def _(i=i):
+                    for t in range(2):
+                        gpr[t, pl.ds(pl.multiple_of(32 * k, 32), 32), :] = gp_stage[2 * i + t]
+
+                @pl.when(i != k)
+                def _(i=i):
+                    remote(
+                        gp_stage.at[pl.ds(2 * i, 2)],
+                        gpr.at[:, pl.ds(pl.multiple_of(32 * k, 32), 32), :],
+                        a2_s.at[0],
+                        a2_r.at[0],
+                        d,
+                        2 * i + c,
+                    ).start()
 
     done = 0
     for j, n in enumerate(turn):
@@ -380,11 +365,13 @@
             halo(n, 0).wait_recv()
 
         ready = NQ if j == NCH - 1 else j * (NQ // NCH)
-        if ready > done:
-            @pl.loop(done, ready)
-            def _(p):
-                finish_quad((turn[0] * (NQ // NCH) + 1 + p) % NQ)
-        done = ready
+        while done < ready:
+            finish_quads([(turn[0] * (NQ // NCH) + 1 + p) % NQ for p in range(done, min(done + 2, ready))])
+            done = min(done + 2, ready)
+        if j == min(1, NCH - 1):
+            for far, dz in ring_i.first:
+                ring_i.take(far, dz)
+                ring_i.share(far, dz)
 
     def slot(f):
         return f // SPD, f % SPD
@@ -519,8 +506,6 @@
             pltpu.VMEM((64, C // 2), BF),
             pltpu.VMEM((DN, 2, 32, 128), BF),
             pltpu.VMEM((3, HN + 2, 32, 128), BF),
-            pltpu.VMEM((3, HN, 96, 128), BF),
-            pltpu.VMEM((3, HN + 1, 96, 128), BF),
             pltpu.VMEM((HN, 32, 128), BF),
             pltpu.VMEM((3, 32, 288), F32),
             pltpu.VMEM((3, 32, 288), BF),

time: 62.2 us -> 59.6 us (0.958)
  the two profiles are of different devices: /device:TPU:2 before, /device:TPU:1 now
where the time goes in v4:
time: 59.6 us; the launch traced here: 59.3 us
  Pallas kernels  56.1 us (94%)
  local copies, waits for them, and re-layouts  2.49 us (4%)
  between operations  0.65 us (1%)
    pallas_call x1, Pallas kernels, shards(): pl.pallas_call(functools.partial(body, DN, C), out_shape=(jax.ShapeDtypeS...  56.1 us
    unnamed x4, local copies, waits for them, and re-layouts  2.49 us

profile of v4, /device:TPU:1, one launch (start us, length us, event | category | flops | bytes accessed | tf_op | source)
XLA Modules:
  0.0 59.3 jit_solution(12709446926509147881)
XLA Ops:
  0.6 56.1 %shard_map.68 = (bf16[128,1024]{1,0:T(8,128)(2,1)}, f32[27,32,32]{2,1,0:T(8,128)}) custom-call(bf16[128,1024]{1,0:T(8,128)(2,1)} %bitcast.6, bf16[64,32,64]{2,1,0:T(8,128)(2,1)} %bitcast.5, bf16[64,1024]{1,0:T(8,128)(2,1)} %wi_hbm.1, bf16[64,1024]{1,0:T(8,128)(2,1)} %wo_hbm.1, bf16[27,32,32]{2,1,0:T(8,128)(2,1)} %kern_hbm.1), custom_call_target="tpu_custom_call" | custom-call | tf_op jit(solution)/shard_map/pallas_call | solution.py:488
  56.8 0.0 copy-start
  56.8 1.7 %copy.9 = bf16[1,2,64,1024]{3,2,1,0:T(8,128)(2,1)} copy(bf16[1,2,64,1024]{3,2,1,0:T(8,128)(2,1)} %bitcast.7) | data formatting | bytes 524288
  58.5 0.0 copy-done
  58.5 0.8 %copy.10 = f32[27,32,32]{2,1,0:T(8,128)} copy(f32[27,32,32]{2,1,0:T(8,128)S(1)} %copy-done) | data formatting | bytes 221184
Async XLA Ops:
  56.8 1.7 %copy-start = (f32[27,32,32]{2,1,0:T(8,128)S(1)}, f32[27,32,32]{2,1,0:T(8,128)}, u32[]{:S(2)}) copy-start(f32[27,32,32]{2,1,0:T(8,128)} %get-tuple-element.9) | copy-start | bytes 331780

commit v5 on v4

--- a/solution.py
+++ b/solution.py
@@ -15,11 +15,10 @@
 def body(
     DN, C,
     go_hbm, pre_hbm, wi_hbm, wo_hbm, kern_hbm,
-    out_hbm, kg_hbm,
     out_ref, kg_ref,
     pre_ref, wi_ref, wo_own, kern_ref, go_buf, wo_buf, wi_buf, wi_own, mt_buf, m_buf, pre2, kmf, kmat, acc, gp_stage, gpr,
     gbuf, g_stage, g_recv, g_fin, p_send, p_recv,
-    in_sem, out_sem, go_sem, gx_s, gx_r, gf_s, gf_r, wo_s, wo_r, wi_s, wi_r, wi_rest, a1_s, a1_r, h_s, h_r, a2_s, a2_r, rs_s, rs_r, ag_s, ag_r, p_s, p_r,
+    in_sem, go_sem, gx_s, gx_r, gf_s, gf_r, wo_s, wo_r, wi_s, wi_r, wi_rest, a1_s, a1_r, h_s, h_r, a2_s, a2_r, rs_s, rs_r, ag_s, ag_r, p_s, p_r,
 ):
     HN = 2 * DN
     Z = DN // 2
@@ -434,7 +433,6 @@
         exchange[n].wait_recv()
         cols = slice(PW * n, PW * (n + 1))
         out_ref[:, cols] = (go_buf[own_cells, cols].astype(F32) + (part + p_recv[n])).astype(BF)
-        pltpu.make_async_copy(out_ref.at[:, cols], out_hbm.at[:, cols], out_sem.at[0]).start()
 
     part = g_fin.at[pl.ds(0, DN - 1)]
     remote(part, part, ag_s.at[0], ag_r.at[0], d, partner).wait_recv()
@@ -446,7 +444,6 @@
         s, m = divmod(o, 9)
         kg_ref[o] = gbuf[s, :, 32 * m : 32 * m + 32]
 
-    pltpu.make_async_copy(kg_ref, kg_hbm, out_sem.at[1]).start()
 
     go_copy.wait_send()
     for there, blocks in ((xh == xl, Z - 1), (across, Z)):
@@ -472,8 +469,6 @@
     left(gp_stage.at[pl.ds(0, 2 * (DN - 1))], a2_s.at[0])
     left(g_stage.at[pl.ds(0, DN - 1)], rs_s.at[0])
     left(g_fin.at[pl.ds(0, DN - 1)], ag_s.at[0])
-    pltpu.make_async_copy(out_ref, out_hbm, out_sem.at[0]).wait()
-    pltpu.make_async_copy(kg_ref, kg_hbm, out_sem.at[1]).wait()
 
 
 def shards(DN, grad_out, pre_act, w_in, w_out, kernel):
@@ -488,14 +483,12 @@
     grad_in, kernel_grad = pl.pallas_call(
         functools.partial(body, DN, C),
         out_shape=(
-            jax.ShapeDtypeStruct((128, C), BF),
-            jax.ShapeDtypeStruct((27, 32, 32), F32),
+            pltpu.VMEM((128, C), BF),
+            pltpu.VMEM((27, 32, 32), F32),
         ),
         in_specs=[pl.BlockSpec(memory_space=pltpu.HBM)] * 5,
-        out_specs=(pl.BlockSpec(memory_space=pl.ANY),) * 2,
+        out_specs=(pl.BlockSpec(memory_space=pltpu.VMEM),) * 2,
         scratch_shapes=[
-            pltpu.VMEM((128, C), BF),
-            pltpu.VMEM((27, 32, 32), F32),
             pltpu.VMEM((2 * HN, 32, 64), BF),
             pltpu.VMEM((64, C), BF),
             pltpu.VMEM((32, C), BF),
@@ -520,7 +513,6 @@
             pltpu.VMEM((np_, 128, C // np_), F32),
             dma((5,)),
             dma((2,)),
-            dma((2,)),
             dma((1,)),
             dma((4,)),
             dma((1,)),

time: 59.6 us -> 57.8 us (0.970)
  local copies, waits for them, and re-layouts: 2.49 us -> 1.47 us
  Pallas kernels: 56.1 us -> 55.4 us
    unnamed x4 -> x2, local copies, waits for them, and re-layouts: 2.49 us -> 1.47 us
    pallas_call x1, Pallas kernels: 56.1 us -> 55.4 us  [shards(): pl.pallas_call(functools.partial(body, DN, C), out_shape=(pltpu.VMEM((128...]
where the time goes in v5:
time: 57.8 us; the launch traced here: 57.5 us
  Pallas kernels  55.4 us (96%)
  local copies, waits for them, and re-layouts  1.47 us (3%)
  between operations  0.64 us (1%)
    pallas_call x1, Pallas kernels, shards(): pl.pallas_call(functools.partial(body, DN, C), out_shape=(pltpu.VMEM((128...  55.4 us
    unnamed x2, local copies, waits for them, and re-layouts  1.47 us

profile of v5, /device:TPU:1, one launch (start us, length us, event | category | flops | bytes accessed | tf_op | source)
XLA Modules:
  0.0 57.5 jit_solution(17264968992121481433)
XLA Ops:
  0.6 55.4 %shard_map.68 = (bf16[128,1024]{1,0:T(8,128)(2,1)S(1)}, f32[27,32,32]{2,1,0:T(8,128)S(1)}) custom-call(bf16[128,1024]{1,0:T(8,128)(2,1)} %bitcast.7, bf16[64,32,64]{2,1,0:T(8,128)(2,1)} %bitcast.6, bf16[64,1024]{1,0:T(8,128)(2,1)} %wi_hbm.1, bf16[64,1024]{1,0:T(8,128)(2,1)} %wo_hbm.1, bf16[27,32,32]{2,1,0:T(8,128)(2,1)} %kern_hbm.1), custom_call_target="tpu_custom_call" | custom-call | tf_op jit(solution)/shard_map/pallas_call | solution.py:483
  56.0 0.7 %copy.9 = bf16[1,2,64,1024]{3,2,1,0:T(8,128)(2,1)} copy(bf16[1,2,64,1024]{3,2,1,0:T(8,128)(2,1)S(1)} %bitcast.5) | data formatting | bytes 524288
  56.7 0.8 %copy.10 = f32[27,32,32]{2,1,0:T(8,128)} copy(f32[27,32,32]{2,1,0:T(8,128)S(1)} %get-tuple-element.7) | data formatting | bytes 221184

commit v6 on v5

--- a/solution.py
+++ b/solution.py
@@ -60,7 +60,8 @@
     pl.semaphore_signal(barrier, inc=1, device_id=(d, partner), device_id_type=MESH)
 
     @pl.loop(1, DN)
-    def _(j):
+    def _(step):
+        j = (step + 3 * DN // 4 - 2) % (DN - 1) + 1
         pl.semaphore_signal(barrier, inc=1, device_id=((d + j) % DN, h), device_id_type=MESH)
         pl.semaphore_signal(barrier, inc=1, device_id=(d, 2 * ((k + j) % DN) + c), device_id_type=MESH)
 
@@ -153,12 +154,8 @@
     def send_block(src, dst, i, to):
         remote(src, dst, wo_s.at[0], wo_r.at[i], *to).start()
 
-    for dz in steps:
+    for dz in steps[:2]:
         send_block(wo_own, wo_buf.at[z], z, served(dz))
-
-    @pl.when(across)
-    def _():
-        send_block(wo_own, wo_buf.at[z], z, served(0))
 
     @pl.when(xh == xl)
     def _():
@@ -224,6 +221,13 @@
         kmf[s, :, 32 * m : 32 * m + 32] = kern_ref[o].astype(F32)
     for s in range(3):
         kmat[s] = kmf[s].astype(BF)
+
+    for dz in steps[2:]:
+        send_block(wo_own, wo_buf.at[z], z, served(dz))
+
+    @pl.when(across)
+    def _():
+        send_block(wo_own, wo_buf.at[z], z, served(0))
 
     @pl.loop(0, HN)
     def _(t):
@@ -363,11 +367,12 @@
         def _(n=n):
             halo(n, 0).wait_recv()
 
-        ready = NQ if j == NCH - 1 else j * (NQ // NCH)
+        ratio = NQ // NCH
+        ready = NQ if j == NCH - 1 else max(0, j * ratio - (ratio == 1))
         while done < ready:
             finish_quads([(turn[0] * (NQ // NCH) + 1 + p) % NQ for p in range(done, min(done + 2, ready))])
             done = min(done + 2, ready)
-        if j == min(1, NCH - 1):
+        if j == NCH // 2:
             for far, dz in ring_i.first:
                 ring_i.take(far, dz)
                 ring_i.share(far, dz)
@@ -476,7 +481,7 @@
     HN = 2 * DN
     rows = grad_out.reshape(128, C)
     turned = jnp.transpose(pre_act, (0, 1, 3, 2)).reshape(2 * HN, 32, 64)
-    nch = max(1, DN // 4)
+    nch = DN // 2
     spd = -(-36 // DN)
     np_ = max(1, C // 256)
     dma = pltpu.SemaphoreType.DMA

time: 57.8 us -> 57.7 us (level)
  no operation moved by 1% of the time
where the time goes in v6:
time: 57.7 us; the launch traced here: 57.5 us
  Pallas kernels  55.4 us (96%)
  local copies, waits for them, and re-layouts  1.47 us (3%)
  between operations  0.64 us (1%)
    pallas_call x1, Pallas kernels, shards(): pl.pallas_call(functools.partial(body, DN, C), out_shape=(pltpu.VMEM((128...  55.4 us
    unnamed x2, local copies, waits for them, and re-layouts  1.47 us

profile of v6, /device:TPU:1, one launch (start us, length us, event | category | flops | bytes accessed | tf_op | source)
XLA Modules:
  0.0 57.5 jit_solution(13509123652523102684)
XLA Ops:
  0.6 55.4 %shard_map.68 = (bf16[128,1024]{1,0:T(8,128)(2,1)S(1)}, f32[27,32,32]{2,1,0:T(8,128)S(1)}) custom-call(bf16[128,1024]{1,0:T(8,128)(2,1)} %bitcast.7, bf16[64,32,64]{2,1,0:T(8,128)(2,1)} %bitcast.6, bf16[64,1024]{1,0:T(8,128)(2,1)} %wi_hbm.1, bf16[64,1024]{1,0:T(8,128)(2,1)} %wo_hbm.1, bf16[27,32,32]{2,1,0:T(8,128)(2,1)} %kern_hbm.1), custom_call_target="tpu_custom_call" | custom-call | tf_op jit(solution)/shard_map/pallas_call | solution.py:488
  56.1 0.7 %copy.9 = bf16[1,2,64,1024]{3,2,1,0:T(8,128)(2,1)} copy(bf16[1,2,64,1024]{3,2,1,0:T(8,128)(2,1)S(1)} %bitcast.5) | data formatting | bytes 524288
  56.8 0.8 %copy.10 = f32[27,32,32]{2,1,0:T(8,128)} copy(f32[27,32,32]{2,1,0:T(8,128)S(1)} %get-tuple-element.7) | data formatting | bytes 221184
